TPU v7x, 256 devices: a whole 4x4x8 slice. The times are simulated.
256 devices in a mesh: rcv: 64 (over x_lo, y, z), ref: 4 (over x_hi, core).
Axes of the slice: x: 4 (x_hi: 2, x_lo: 2; x = x_hi * 2 + x_lo), y: 4, z: 8, core: 2. Of those that a mesh axis runs over, the one named last changes fastest.
Arguments:
- receiver_spectra: bfloat16 [512, 8192], P('rcv', 'ref'), may hold values from -6 to 6
- reference_spectra: bfloat16 [8192, 1024], P('rcv', 'ref'), may hold values from -6 to 6
- receiver_counts: int32 [512], P('rcv'), may hold values from 1 to 16
- reference_counts: int32 [1024], P('ref'), may hold values from 1 to 16
- column_station: int32 [1024], P('ref'), may hold values from 0 to 1023, as said below
- lag_window: int32 [2, 512, 1024], P(None, 'rcv', 'ref'), may hold values from 0 to 256, as said below
- observed: bfloat16 [512, 1024, 512], P('rcv', 'ref'), may hold values from 0.19921875 to 2
Outputs:
- receiver_grad: float32 [512, 8192], P('rcv', 'ref')
- reference_grad: float32 [8192, 1024], P('rcv', 'ref')
Inputs may be any that keep to these rules, and one draw needn't show every extreme that they name: `receiver_counts`: number of valid leading segments of each station. `column_station`: A permutation of the 1024 reference stations that maps each block of 256 consecutive pair columns onto the same block of stations. lag_window[0] is a first lag below 256; lag_window[1] is a number of lags from 64 to 256.
All inputs are finite; a program needn't handle non-finite values.
Results may differ from a plain program's by a relative error of at most 0.0014.
Values may be sent and summed in bfloat16 or wider, within the bound.
A program may use at most 64 MiB of HBM per device.

v0:
```python
import math

import jax
import jax.numpy as jnp
from jax import lax
from jax.sharding import Mesh
from jax.sharding import PartitionSpec as P

L = 512
S = 16
F = 256
K = 8192
RCV = ("rcv_0", "rcv_1", "rcv_2")


env_floor = 0.05
misfit_scale = 0.03125


def copy_for_each(shard, axis):
    copies = jnp.broadcast_to(shard, (lax.axis_size(axis), *shard.shape))
    return lax.all_to_all(copies, axis, split_axis=0, concat_axis=0, tiled=True)


def joined_along(parts, dim):
    parts = jnp.moveaxis(parts, 0, dim)
    dims = parts.shape
    return parts.reshape(*dims[:dim], dims[dim] * dims[dim + 1], *dims[dim + 2 :])


def gathered_copies(shard, axis, dim):
    parts = copy_for_each(shard, axis)
    return joined_along(parts, dim)


def all_blocks(shard, axes, order):
    parts = shard[None]
    for k in order:
        parts = lax.all_gather(parts, axes[k], axis=0, tiled=True)
    block = [lax.axis_size(axes[k]) for k in reversed(order)]
    parts = parts.reshape(*block, *shard.shape)
    turned = sorted(range(len(order)), key=lambda place: order[len(order) - 1 - place])
    return parts.transpose(*turned, *range(len(order), parts.ndim)).reshape(-1, *shard.shape)


def gather_axes(shard, axes, order, dim):
    return joined_along(all_blocks(shard, axes, order), dim)


def in_blocks(shard, dim, size):
    before, after = (shard.shape[:dim], shard.shape[dim + 1 :])
    return jnp.moveaxis(shard.reshape(*before, size, -1, *after), dim, 0)


def summed_on_arrival(shard, axis, dim):
    size = lax.axis_size(axis)
    parts = lax.all_to_all(in_blocks(shard, dim, size), axis, 0, 0, tiled=True)
    return jnp.sum(parts, axis=0)


def sent_together(arrays, axis, split_dim, concat_dim, along):
    both = jnp.concatenate(arrays, axis=along)
    whole, at, outs = (
        lax.all_to_all(both, axis, split_axis=split_dim, concat_axis=concat_dim, tiled=True),
        0,
        [],
    )
    for a in arrays:
        outs.append(lax.slice_in_dim(whole, at, at + a.shape[along], axis=along))
        at += a.shape[along]
    return tuple(outs)


def lag_table(freq_total, lag_total):
    freq_ids = jnp.arange(freq_total, dtype=jnp.int32)[:, None]
    lag_ids = jnp.arange(lag_total, dtype=jnp.int32)[None, :] - lag_total // 2
    phase_ids = freq_ids * lag_ids % lag_total
    phase_angle = phase_ids.astype(jnp.float32) * (2.0 * math.pi / lag_total)
    cosine = jnp.cos(phase_angle) / math.sqrt(freq_total)
    sine_part = jnp.sin(phase_angle) / math.sqrt(freq_total)
    real_rows = jnp.concatenate([cosine, sine_part], axis=1)
    imag_rows = jnp.concatenate([-sine_part, cosine], axis=1)
    stacked = jnp.stack([real_rows, imag_rows], axis=1)
    return stacked.reshape(2 * freq_total, 2 * lag_total).astype(jnp.bfloat16)


def segment_masks(receiver_counts, pair_counts, seg_total):
    seg_ids = jnp.arange(seg_total, dtype=jnp.int32)
    receiver_mask = (seg_ids[None, :] < receiver_counts[:, None]).astype(jnp.float32)
    reference_mask = (seg_ids[:, None] < pair_counts[None, :]).astype(jnp.float32)
    return (receiver_mask, reference_mask)


def receiver_operand(receiver_vals):
    real_part = receiver_vals[:, :, 0, :]
    imag_part = receiver_vals[:, :, 1, :]
    first_row = jnp.concatenate([real_part, imag_part], axis=-1)
    second_row = jnp.concatenate([imag_part, -real_part], axis=-1)
    return jnp.stack([first_row, second_row], axis=2)


def reference_operand(reference_vals):
    real_part = reference_vals[:, 0]
    imag_part = reference_vals[:, 1]
    first_row = jnp.stack([real_part, imag_part], axis=1)
    second_row = jnp.stack([-imag_part, real_part], axis=1)
    return jnp.stack([first_row, second_row], axis=1)


def shards(
    receiver_spectra,
    reference_spectra,
    receiver_counts,
    reference_counts,
    column_station,
    lag_window,
    observed,
):
    row_total = receiver_spectra.shape[0]
    col_total = reference_spectra.shape[1]
    lag_matrix = lag_table(F, L)
    whole_receiver = gathered_copies(receiver_spectra, "ref", 1)
    whole_reference = gather_axes(reference_spectra, RCV, (0, 1, 2), 0)
    local_order = column_station - lax.axis_index("ref") * col_total
    pair_counts = jnp.take(reference_counts, local_order)
    receiver_mask, reference_mask = segment_masks(receiver_counts, pair_counts, S)
    receiver_vals = whole_receiver.reshape(row_total, F, 2, S) * receiver_mask[
        :, None, None, :
    ].astype(jnp.bfloat16)
    reference_vals = jnp.take(whole_reference, local_order, axis=1).reshape(F, 2, S, col_total)
    reference_vals = reference_vals * reference_mask[None, None, :, :].astype(jnp.bfloat16)
    receiver_op = receiver_operand(receiver_vals)
    pair_norm = jnp.minimum(receiver_counts[:, None], pair_counts[None, :]).astype(jnp.float32)
    cross_spec = jnp.einsum(
        "ifqk,fkj->ijfq",
        receiver_op,
        reference_vals.reshape(F, 2 * S, col_total),
        preferred_element_type=jnp.float32,
    )
    spectra = (cross_spec / pair_norm[:, :, None, None]).astype(jnp.bfloat16)
    lagged = jnp.dot(
        spectra.reshape(row_total * col_total, 2 * F),
        lag_matrix,
        preferred_element_type=jnp.float32,
    )
    lagged = lagged.reshape(row_total, col_total, 2 * L)
    correlation = lagged[..., :L]
    hilbert_part = lagged[..., L:]
    envelope = jnp.sqrt(correlation * correlation + hilbert_part * hilbert_part + env_floor)
    lag_ids = jnp.arange(L, dtype=jnp.int32)
    inside = (lag_ids >= lag_window[0][..., None]) & (
        lag_ids < (lag_window[0] + lag_window[1])[..., None]
    )
    misfit = jnp.where(inside, envelope - observed.astype(jnp.float32), 0.0) * misfit_scale
    weights = jnp.concatenate(
        [misfit * correlation / envelope, misfit * hilbert_part / envelope], axis=-1
    ).astype(jnp.bfloat16)
    back_proj = lax.dot_general(
        weights.reshape(row_total * col_total, 2 * L),
        lag_matrix,
        (((1,), (1,)), ((), ())),
        preferred_element_type=jnp.float32,
    )
    back_proj = back_proj.reshape(row_total, col_total, F, 2)
    grad_spec = (back_proj / pair_norm[:, :, None, None]).astype(jnp.bfloat16)
    receiver_part = jnp.einsum(
        "ijfq,fqcsj->ifcs",
        grad_spec,
        reference_operand(reference_vals),
        preferred_element_type=jnp.float32,
    )
    receiver_part = receiver_part * receiver_mask[:, None, None, :]
    receiver_grad = summed_on_arrival(receiver_part.reshape(row_total, K), "ref", 1)
    inverse_order = (
        jnp.zeros((col_total,), jnp.int32)
        .at[local_order]
        .set(jnp.arange(col_total, dtype=jnp.int32))
    )
    sent_grad = jnp.transpose(grad_spec, (0, 2, 3, 1)).reshape(row_total, F, 2 * col_total)
    sent_op = receiver_op.reshape(row_total, F, 4 * S)
    got_grad, got_op = sent_together((sent_grad, sent_op), RCV, 1, 0, 2)
    freq_span = got_grad.shape[1]
    term_block = jnp.einsum(
        "ifqj,ifqk->fkj",
        got_grad.reshape(-1, freq_span, 2, col_total),
        got_op.reshape(-1, freq_span, 2, 2 * S),
        preferred_element_type=jnp.float32,
    )
    term_block = term_block.reshape(freq_span, 2, S, col_total) * reference_mask[None, None, :, :]
    reference_grad = jnp.take(
        term_block.reshape(freq_span * 2 * S, col_total), inverse_order, axis=1
    )
    return (receiver_grad, reference_grad)


def solution(mesh):
    finer = Mesh(
        mesh.devices.reshape(2, 4, 8, mesh.shape["ref"]), ("rcv_0", "rcv_1", "rcv_2", "ref")
    )
    placed = (
        P(RCV, "ref"),
        P(RCV, "ref"),
        P(RCV),
        P("ref"),
        P("ref"),
        P(None, RCV, "ref"),
        P(RCV, "ref", None),
    )
    return jax.shard_map(
        shards,
        mesh=finer,
        in_specs=placed,
        out_specs=(P(RCV, "ref"), P(RCV, "ref")),
        check_vma=False,
    )
```

profile of v0, /device:TPU:34, one launch (start us, length us, event | category | flops | bytes accessed | tf_op | source)
XLA Modules:
  0.0 263.4 jit_solution(12746543526087631553)
XLA Ops:
  7.2 5.1 %all-gather = bf16[256,256]{1,0:T(8,128)(2,1)S(1)} all-gather(bf16[128,256]{1,0:T(8,128)(2,1)} %param.8), channel_id=2, replica_groups=mesh['rcv_0'=2,'rcv_1'=4,'rcv_2'=8,'ref'=4] {'rcv_0'}, dimensions={0}, use_global_device_ids=true | all-gather | bytes 196608 | tf_op jit(solution)/shard_map/all_gather | solution.py:39
  12.4 14.2 %all_gather.10 = bf16[8,128,256]{2,1,0:T(8,128)(2,1)} all-gather(bf16[2,128,256]{2,1,0:T(8,128)(2,1)S(1)} %bitcast.112), channel_id=1, replica_groups=mesh['rcv_0'=2,'rcv_1'=4,'rcv_2'=8,'ref'=4] {'rcv_1'}, dimensions={0}, use_global_device_ids=true | all-gather | bytes 655360 | tf_op jit(solution)/shard_map/all_gather | solution.py:39
  26.6 1.4 broadcast_in_dim.75
  28.1 3.4 %all-to-all-start = ((bf16[4,8,2048]{2,1,0:T(8,128)(2,1)}), bf16[4,8,2048]{2,1,0:T(8,128)(2,1)S(1)}, u32[]{:S(2)}, u32[]{:S(2)}) async-start(bf16[4,8,2048]{2,1,0:T(8,128)(2,1)} %broadcast_in_dim.75), calls=%async_computation | async-start | bytes 262144 | tf_op jit(solution)/shard_map/all_to_all | solution.py:22
  32.1 1.9 gather_fusion.1
  37.7 2.3 fusion.30
  41.0 0.9 broadcast_multiply_fusion
  41.9 1.5 fusion.41
  45.1 36.7 %all-gather.3.cloned.1.call-done = bf16[64,128,256]{2,1,0:T(8,128)(2,1)} async-done(((bf16[8,128,256]{2,1,0:T(8,128)(2,1)}), bf16[64,128,256]{2,1,0:T(8,128)(2,1)}) %all-gather.3.cloned.1.call-update) | async-done | bytes 4194320 | tf_op jit(solution)/shard_map/all_gather | solution.py:39
  81.8 8.5 %copy.99 = bf16[2,4,8,128,256]{3,2,1,0,4:T(8,128)(2,1)} copy(bf16[2,4,8,128,256]{4,3,0,1,2:T(8,128)(2,1)} %bitcast.102) | data formatting | bytes 8388608 | tf_op jit(solution)/shard_map/transpose | solution.py:43
  90.2 12.3 %copy.133 = bf16[32,8,64,128]{3,1,2,0:T(8,128)(2,1)} copy(bf16[32,8,64,128]{3,2,1,0:T(8,128)(2,1)} %bitcast.95) | data formatting | bytes 8388608
  102.5 11.9 %gather_fusion = bf16[256,8192]{1,0:T(8,128)(2,1)} fusion(bf16[8192,256]{0,1:T(8,128)(2,1)} %bitcast.91, s32[1024]{0:T(1024)S(1)} %pad_clamp_fusion.1), kind=kCustom, calls=%fused_computation | custom fusion | bytes 8389632 | tf_op jit(solution)/shard_map/jit(_take)/gather | solution.py:130
  114.4 6.4 %copy.100 = bf16[8192,256]{1,0:T(8,128)(2,1)} copy(bf16[8192,256]{0,1:T(8,128)(2,1)} %bitcast.96) | data formatting | bytes 8388608 | tf_op jit(solution)/shard_map/jit(_take)/gather | solution.py:130
  120.8 3.6 %fusion.9 = bf16[8,256,256,2]{1,0,3,2:T(8,128)(2,1)S(1)} fusion(f32[8,256]{1,0:T(8,128)S(1)} %minimum_convert_fusion, bf16[256,32,256]{2,1,0:T(8,128)(2,1)} %bitcast.92, pred[256]{0:T(512)(128)(4,1)S(1)} %get-tuple-element.15, bf16[32,256]{1,0:T(8,128)(2,1)S(1)} %bitcast.116, bf16[8,256,1,32]{3,0,2,1:T(8,128)(2,1)S(1)} %bitcast.105, ...), kind=kOutput, calls=%fused_computation.17 | convolution fusion | flops 80216064 | bytes 6578432 | tf_op jit(solution)/shard_map/ifqk,fkj->ijfq/dot_general | solution.py:134
  124.3 2.9 %convolution_bitcast_fusion = f32[8,256,1024]{2,1,0:T(8,128)S(1)} fusion(bf16[8,256,256,2]{1,0,3,2:T(8,128)(2,1)S(1)} %fusion.9, bf16[256,1,1024]{2,0,1:T(8,128)(2,1)S(1)} %get-tuple-element.23, bf16[256,1,1024]{2,0,1:T(8,128)(2,1)S(1)} %get-tuple-element.22), kind=kOutput, calls=%fused_computation.31 | convolution fusion | flops 2148007936 | bytes 11534336 | tf_op jit(solution)/shard_map/dot_general | solution.py:141
  127.3 4.0 %divide_convert_fusion.2 = (bf16[8,256,512]{2,1,0:T(8,128)(2,1)S(1)}, bf16[8,256,512]{2,1,0:T(8,128)(2,1)S(1)}) fusion(bf16[8,256,512]{2,1,0:T(8,128)(2,1)S(1)} %copy-done.5, f32[8,256,1024]{2,1,0:T(8,128)S(1)} %convolution_bitcast_fusion, s32[8,256]{1,0:T(8,128)S(1)} %bitcast_add_fusion, s32[8,256]{1,0:T(8,128)S(1)} %slice_bitcast_fusion), kind=kLoop, calls=%fused_computation.20 | loop fusion | flops 17825792 | bytes 14696448 | tf_op jit(solution)/shard_map/convert
  131.3 4.4 %fusion.4 = f32[8,256,256,2]{2,1,3,0:T(8,128)} fusion(bf16[8,256,512]{2,1,0:T(8,128)(2,1)S(1)} %get-tuple-element.17, bf16[8,256,512]{2,1,0:T(8,128)(2,1)S(1)} %get-tuple-element.16, bf16[256,1,1024]{2,0,1:T(8,128)(2,1)S(1)} %get-tuple-element.23, bf16[256,1,1024]{2,0,1:T(8,128)(2,1)S(1)} %get-tuple-element.22), kind=kOutput, calls=%fused_computation.11 | convolution fusion | flops 2157969408 | bytes 9437184 | tf_op jit(solution)/shard_map/dot_general | solution.py:158
  135.7 5.7 %copy.109 = f32[8,256,256,2]{1,0,3,2:T(8,128)} copy(f32[8,256,256,2]{2,1,3,0:T(8,128)} %fusion.4) | data formatting | bytes 8388608 | tf_op jit(solution)/shard_map/dot_general | solution.py:158
  141.4 2.9 %divide_convert_fusion = bf16[8,256,256,2]{1,0,3,2:T(8,128)(2,1)S(1)} fusion(f32[8,256,256,2]{1,0,3,2:T(8,128)} %copy.109, f32[8,256]{1,0:T(8,128)S(1)} %minimum_convert_fusion), kind=kLoop, calls=%fused_computation.18 | loop fusion | flops 2097152 | bytes 6299648 | tf_op jit(solution)/shard_map/convert_element_type | solution.py:165
  146.3 9.8 %bitcast_multiply_fusion = f32[8,256,2,16]{3,0,2,1:T(8,128)S(1)} fusion(bf16[8,256,256,2]{1,0,3,2:T(8,128)(2,1)S(1)} %divide_convert_fusion, bf16[256,1,2,16,256]{4,3,1,2,0:T(8,128)(2,1)S(1)} %maximum_bitcast_fusion, bf16[256,1,2,16,256]{4,3,1,2,0:T(8,128)(2,1)S(1)} %select_multiply_fusion.2, f32[8,16]{1,0:T(8,128)S(1)} %get-tuple-element.31), kind=kOutput, calls=%fused_computation.35 | convolution fusion | flops 71368704 | bytes 10748416 | tf_op jit(solution)/shard_map/ijfq,fqcsj->ifcs/dot_general | solution.py:166
  156.1 2.4 copy.110
  158.5 4.3 %reshape_reshape.11 = f32[8,4,2048]{2,1,0:T(4,128)S(1)} reshape(f32[8,256,2,16]{3,2,1,0:T(2,128)} %copy.110) | data formatting | bytes 524288 | tf_op jit(solution)/shard_map/reshape;reshape | solution.py:52
  163.6 4.3 %all-to-all-start.1 = ((f32[4,8,2048]{2,1,0:T(8,128)}), f32[4,8,2048]{2,1,0:T(8,128)}, u32[]{:S(2)}, u32[]{:S(2)}) async-start(f32[4,8,2048]{2,1,0:T(8,128)} %copy.111), calls=%async_computation.1 | async-start | bytes 524288 | tf_op jit(solution)/shard_map/all_to_all | solution.py:57
  167.9 1.4 pad_maximum_fusion.1
  170.6 1.7 pad_maximum_fusion
  172.3 3.2 %all-to-all-done.1 = f32[4,8,2048]{2,1,0:T(8,128)} async-done(((f32[4,8,2048]{2,1,0:T(8,128)}), f32[4,8,2048]{2,1,0:T(8,128)}, u32[]{:S(2)}, u32[]{:S(2)}) %all-to-all-start.1) | async-done | bytes 262176 | tf_op jit(solution)/shard_map/all_to_all | solution.py:57
  175.5 10.6 %all-to-all-start.2 = ((bf16[8,256,576]{2,0,1:T(8,128)(2,1)}), bf16[8,256,576]{2,0,1:T(8,128)(2,1)S(1)}, u32[]{:S(2)}, u32[]{:S(2)}) async-start(bf16[8,256,576]{2,0,1:T(8,128)(2,1)} %pad_maximum_fusion), calls=%async_computation.2 | async-start | bytes 5242880 | tf_op jit(solution)/shard_map/all_to_all | solution.py:64
  186.2 1.4 scatter_custom_fusion
  187.7 1.6 reduce_sum.9
  189.3 59.7 %all-to-all-done.2 = bf16[8,256,576]{2,0,1:T(8,128)(2,1)S(1)} async-done(((bf16[8,256,576]{2,0,1:T(8,128)(2,1)}), bf16[8,256,576]{2,0,1:T(8,128)(2,1)S(1)}, u32[]{:S(2)}, u32[]{:S(2)}) %all-to-all-start.2) | async-done | bytes 2359328 | tf_op jit(solution)/shard_map/all_to_all | solution.py:64
  249.2 1.5 slice.55
  250.8 2.8 %copy.116 = bf16[512,4,512]{0,2,1:T(8,128)(2,1)S(1)} copy(bf16[512,4,512]{2,0,1:T(8,128)(2,1)} %slice.55) | data formatting | bytes 4194304 | tf_op jit(solution)/shard_map/slice | solution.py:69
  (56 shorter events, 14.0 us)
Async XLA Ops:
  7.2 25.0 %copy-start = (s32[256]{0:T(256)S(1)}, s32[256]{0:T(256)}, u32[]{:S(2)}) copy-start(s32[256]{0:T(256)} %param.10) | copy-start | bytes 3076
  7.2 74.6 %all-gather.3.cloned.1.call-start = ((), (), s32[]{:S(2)}) async-start(), calls=%async_computation.3 | async-start | bytes 4718592 | tf_op jit(solution)/shard_map/all_gather | solution.py:39
  28.1 12.0 %all-to-all-start = ((bf16[4,8,2048]{2,1,0:T(8,128)(2,1)}), bf16[4,8,2048]{2,1,0:T(8,128)(2,1)S(1)}, u32[]{:S(2)}, u32[]{:S(2)}) async-start(bf16[4,8,2048]{2,1,0:T(8,128)(2,1)} %broadcast_in_dim.75), calls=%async_computation | async-start | bytes 262144 | tf_op jit(solution)/shard_map/all_to_all | solution.py:22
  44.7 76.0 %copy-start.3 = (bf16[8,256,32]{2,0,1:T(8,128)(2,1)}, bf16[8,256,32]{2,0,1:T(8,128)(2,1)S(1)}, u32[]{:S(2)}) copy-start(bf16[8,256,32]{2,0,1:T(8,128)(2,1)S(1)} %copy.106) | copy-start | bytes 393220
  45.1 75.7 %copy-start.4 = (bf16[8,256,32]{2,0,1:T(8,128)(2,1)}, bf16[8,256,32]{2,0,1:T(8,128)(2,1)S(1)}, u32[]{:S(2)}) copy-start(bf16[8,256,32]{2,0,1:T(8,128)(2,1)S(1)} %copy.107) | copy-start | bytes 393220
  124.3 2.9 %copy-start.5 = (bf16[8,256,512]{2,1,0:T(8,128)(2,1)S(1)}, bf16[8,256,512]{2,1,0:T(8,128)(2,1)}, u32[]{:S(2)}) copy-start(bf16[8,256,512]{2,1,0:T(8,128)(2,1)} %param.13) | copy-start | bytes 6291460
  141.4 3.5 %copy-start.2 = (bf16[8192,256]{1,0:T(8,128)(2,1)S(1)}, bf16[8192,256]{1,0:T(8,128)(2,1)}, u32[]{:S(2)}) copy-start(bf16[8192,256]{1,0:T(8,128)(2,1)} %copy.100) | copy-start | bytes 12582916
  163.6 11.8 %all-to-all-start.1 = ((f32[4,8,2048]{2,1,0:T(8,128)}), f32[4,8,2048]{2,1,0:T(8,128)}, u32[]{:S(2)}, u32[]{:S(2)}) async-start(f32[4,8,2048]{2,1,0:T(8,128)} %copy.111), calls=%async_computation.1 | async-start | bytes 524288 | tf_op jit(solution)/shard_map/all_to_all | solution.py:57
  175.5 73.4 %all-to-all-start.2 = ((bf16[8,256,576]{2,0,1:T(8,128)(2,1)}), bf16[8,256,576]{2,0,1:T(8,128)(2,1)S(1)}, u32[]{:S(2)}, u32[]{:S(2)}) async-start(bf16[8,256,576]{2,0,1:T(8,128)(2,1)} %pad_maximum_fusion), calls=%async_computation.2 | async-start | bytes 5242880 | tf_op jit(solution)/shard_map/all_to_all | solution.py:64
  250.7 5.6 %copy-start.1 = (s32[256]{0:T(256)S(1)}, s32[256]{0:T(256)}, u32[]{:S(2)}) copy-start(s32[256]{0:T(256)} %param.10) | copy-start | bytes 3076
Sparse Core Ops, SparseCore 0:
  26.8 54.9 all-gather.2
where the time goes:
time: 269 us; the launch traced here: 263 us
  waiting for transfers between devices  99.5 us (37%)
  local copies, waits for them, and re-layouts  69.9 us (26%)
  matrix products  21.4 us (8%)
  other arithmetic  20.1 us (7%)
  blocking collectives  19.4 us (7%)
  starting transfers between devices  18.3 us (7%)
  between operations  14.7 us (5%)
    all_to_all x1, waiting for transfers between devices, sent_together(): lax.all_to_all(both, axis, split_axis=split_dim, concat_axis=concat_dim,...  59.7 us
    all_gather x1, waiting for transfers between devices, all_blocks(): parts = lax.all_gather(parts, axes[k], axis=0, tiled=True)  36.7 us
    all_gather x2, blocking collectives, all_blocks(): parts = lax.all_gather(parts, axes[k], axis=0, tiled=True)  19.4 us
    gather x2, local copies, waits for them, and re-layouts, shards(): jnp.take(whole_reference, local_order, axis=1).reshape(F, 2, S, col_total)  18.2 us
    unnamed x14, local copies, waits for them, and re-layouts  13.6 us
    all_to_all x1, starting transfers between devices, sent_together(): lax.all_to_all(both, axis, split_axis=split_dim, concat_axis=concat_dim,...  10.6 us
    dot_general x1, matrix products, shards(): jnp.einsum('ijfq,fqcsj->ifcs', grad_spec, reference_operand(reference_val...  9.84 us
    transpose x1, local copies, waits for them, and re-layouts, all_blocks(): parts.transpose(*turned, *range(len(order), parts.ndim))  8.45 us
  transfers between devices with their start and end apart: 4, of which 3 were waited for; matrix products, arithmetic and copies ran while one was open for 9% of the time, Pallas kernels for 0%

commit v1 on v0

v1 whole, which is shorter than its diff:
```python
import functools
import math

import jax
import jax.numpy as jnp
import numpy as np
from jax import lax
from jax.experimental import pallas as pl
from jax.experimental.pallas import tpu as pltpu
from jax.sharding import PartitionSpec as P

L = 512
S = 16
F = 256
NP = 8
NZ = 8
NI = 8
NJ = 256
NG = 4
MESH = pl.DeviceIdType.MESH
BF = jnp.bfloat16
F32 = jnp.float32

env_floor = 0.05
misfit_scale = 0.03125


def lag_table():
    freq_ids = np.arange(F, dtype=np.int64)[:, None]
    lag_ids = np.arange(L, dtype=np.int64)[None, :] - L // 2
    angle = ((freq_ids * lag_ids) % L).astype(np.float64) * (2.0 * math.pi / L)
    cosine = np.cos(angle) / math.sqrt(F)
    sine = np.sin(angle) / math.sqrt(F)
    real_rows = np.concatenate([cosine, sine], axis=1)
    imag_rows = np.concatenate([-sine, cosine], axis=1)
    stacked = np.stack([real_rows, imag_rows], axis=1).reshape(2 * F, 2 * L)
    return stacked.astype(np.float32)


def kernel(
    u_ref, v_ref, rc_ref, fc_ref, cs_ref, win_ref, obs_ref, m_ref, mt_ref,
    rg_out, wg_out,
    um, us, vg, bt, bb, rinv, ninv, obst, xs, xr, gs, zs, zr, w, rbuf, lbuf, rgp, rgr,
    u_send, u_recv, v_send, v_recv, x_send, x_recv, z_send, z_recv,
    g_send, g_recv, r_send, r_recv, l_send, l_recv, own_sem,
):
    r = lax.axis_index("rcv")
    q = lax.axis_index("ref")
    p = r // NZ
    z = r % NZ

    def signal(rr, qq):
        pl.semaphore_signal(barrier, inc=1, device_id=(rr, qq), device_id_type=MESH)

    def remote(src, dst, send, recv, rr, qq):
        return pltpu.make_async_remote_copy(
            src_ref=src, dst_ref=dst, send_sem=send, recv_sem=recv,
            device_id=(rr, qq), device_id_type=MESH,
        )

    def plane(k):
        return ((p + k) % NP) * NZ + z

    def wait_bytes(ref, sem):
        pltpu.make_async_copy(ref, ref, sem).wait()

    barrier = pltpu.get_barrier_semaphore()
    for k in range(1, NP):
        signal(plane(k), q)
    for k in range(1, NZ):
        signal(p * NZ + (z + k) % NZ, q)
    for k in range(NP):
        own = jnp.logical_and(k == 0, p // 2 == q)

        @pl.when(jnp.logical_not(own))
        def _():
            signal(plane(k), p // 2)

    for half in range(2):
        for qq in range(4):
            rr = (2 * q + half) * NZ + z
            own = jnp.logical_and(rr == r, qq == q)

            @pl.when(jnp.logical_not(own))
            def _():
                signal(rr, qq)

    order = cs_ref[...] - q * NJ
    stations = lax.broadcasted_iota(jnp.int32, (NJ, NJ), 0)
    onehot = jnp.where(stations == order, 1.0, 0.0)
    onehot_b = onehot.astype(BF)
    counts8 = jnp.broadcast_to(fc_ref[...].astype(F32), (8, NJ)).astype(BF)
    pc = jnp.dot(counts8, onehot_b, preferred_element_type=F32)[0:1, :]
    seg_row = lax.broadcasted_iota(jnp.int32, (128, NJ), 0) % S
    row_mask = seg_row.astype(F32) < pc
    vp = jnp.dot(v_ref[...], onehot_b, preferred_element_type=F32)
    vg[z] = jnp.where(row_mask, vp, 0.0).astype(BF)
    seg_lane = lax.broadcasted_iota(jnp.int32, (NI, 2048), 1) % S
    rcounts = rc_ref[...]
    masked = jnp.where(seg_lane < rcounts, u_ref[...].astype(F32), 0.0).astype(BF)
    tail = jnp.broadcast_to(rcounts.astype(F32), (NI, 128)).astype(BF)
    for half in range(2):
        um[half, :, 0:1024] = masked[:, half * 1024 : (half + 1) * 1024]
        um[half, :, 1024:1152] = tail
    ninv[...] = 1.0 / jnp.minimum(rcounts.astype(F32), pc)

    mine = jnp.where(p // 2 == q, 2, 0)
    pl.semaphore_wait(barrier, 2 * (NP - 1) + 2 * NP - mine)

    for half in range(2):
        for qq in range(4):
            pp = 2 * q + half
            rr = pp * NZ + z
            own = jnp.logical_and(rr == r, qq == q)
            slot = (p - pp + NP) % NP

            @pl.when(jnp.logical_not(own))
            def _():
                remote(um.at[half], us.at[slot], u_send.at[half, qq], u_recv.at[slot], rr, qq).start()

            @pl.when(own)
            def _():
                pltpu.make_async_copy(um.at[half], us.at[slot], u_recv.at[slot]).start()

    for k in (1, 7, 2, 6, 3, 5, 4):
        remote(vg.at[z], vg.at[z], v_send.at[k], v_recv.at[z], p * NZ + (z + k) % NZ, q).start()

    def turn(i, c):
        obst[i] = jnp.transpose(obs_ref[i].astype(F32), (1, 0)).astype(BF)
        return c

    lax.fori_loop(0, NI, turn, 0)

    row16 = lax.broadcasted_iota(jnp.int32, (16, 256), 0)
    lane256 = lax.broadcasted_iota(jnp.int32, (16, 256), 1)
    diag = (lane256 // 32) == (row16 // 2)
    mask0 = jnp.logical_and(diag, row16 % 2 == 0)
    mask1 = jnp.logical_and(diag, row16 % 2 == 1)

    def operand(k, c):
        wait_bytes(us.at[k], u_recv.at[k])
        uf = us[k, :, 0:1024].astype(F32)
        part = (lax.broadcasted_iota(jnp.int32, (NI, 1024), 1) // S) % 2
        turned = jnp.where(part == 0, pltpu.roll(uf, 1024 - S, 1), -pltpu.roll(uf, S, 1))
        rinv[k] = 1.0 / jnp.minimum(us[k, :, 1024:1025].astype(F32), pc)
        for g in range(NG):
            a = uf[:, g * 256 : (g + 1) * 256]
            b = turned[:, g * 256 : (g + 1) * 256]
            for i in range(NI):
                blk = jnp.where(mask0, a[i : i + 1], jnp.where(mask1, b[i : i + 1], 0.0))
                bt[g, i, pl.ds(k * 16, 16), :] = blk.astype(BF)
        return c

    lax.fori_loop(0, NP, operand, 0)

    for k in range(1, NZ):
        zz = (z + k) % NZ
        wait_bytes(vg.at[zz], v_recv.at[zz])

    def cross(i, c):
        scale = jnp.concatenate(
            [jnp.broadcast_to(rinv[k, pl.ds(i, 1), :], (16, NJ)) for k in range(NP)], axis=0
        )
        for g in range(NG):
            block = vg[2 * g : 2 * g + 2].reshape(256, NJ)
            x = jnp.dot(bt[g, i], block, preferred_element_type=F32) * scale
            x = x.astype(BF)
            xr[i, p, g * 16 : (g + 1) * 16, :] = x[0:16]
            for k in range(1, NP):
                xs[i, k, g * 16 : (g + 1) * 16, :] = x[k * 16 : (k + 1) * 16]
        for k in range(1, NP):
            remote(xs.at[i, k], xr.at[i, p], x_send.at[i], x_recv.at[i], plane(k), q).start()
        return c

    lax.fori_loop(0, NI, cross, 0)

    def flip(g, c):
        for i in range(0, NI, 2):
            both = bt[g, i : i + 2].reshape(256, 256).astype(F32)
            bb[g, :, i * 128 : (i + 2) * 128] = jnp.transpose(both, (1, 0)).astype(BF)
        return c

    lax.fori_loop(0, NG, flip, 0)

    TB = 128

    def pairs(i, c):
        wait_bytes(xs.at[i, 1:NP], x_recv.at[i])
        x = xr[i].reshape(2 * F, NJ)
        first = win_ref[0, pl.ds(i, 1), :]
        last = first + win_ref[1, pl.ds(i, 1), :]
        for b in range(L // TB):
            cor = jnp.dot(mt_ref[b * TB : (b + 1) * TB, :], x, preferred_element_type=F32)
            hil = jnp.dot(mt_ref[L + b * TB : L + (b + 1) * TB, :], x, preferred_element_type=F32)
            rs = lax.rsqrt(cor * cor + hil * hil + env_floor)
            lag = lax.broadcasted_iota(jnp.int32, (TB, NJ), 0) + b * TB
            inside = jnp.logical_and(lag >= first, lag < last)
            seen = obst[i, b * TB : (b + 1) * TB, :].astype(F32)
            wt = jnp.where(inside, (1.0 - seen * rs) * misfit_scale, 0.0)
            gs[b * TB : (b + 1) * TB, :] = (wt * cor).astype(BF)
            gs[L + b * TB : L + (b + 1) * TB, :] = (wt * hil).astype(BF)
        scale = ninv[pl.ds(i, 1), :]
        for b in range(4):
            back = jnp.dot(m_ref[b * 128 : (b + 1) * 128, :], gs[...], preferred_element_type=F32)
            zs[i, 2 * b : 2 * b + 2] = (back * scale).astype(BF).reshape(2, NG, 16, NJ)
        for k in range(1, NP):
            remote(
                zs.at[i, (p + k) % NP], zr.at[:, i, NP - k], z_send.at[i], z_recv.at[i], plane(k), q
            ).start()
        zr[:, i, 0] = zs[i, p]
        return c

    lax.fori_loop(0, NI, pairs, 0)

    lane8 = (lax.broadcasted_iota(jnp.int32, (NP, 256), 1) // S) % 2

    def receivers(i, c):
        wait_bytes(zs.at[i, 1:NP], z_recv.at[i])
        for g in range(NG):
            block = vg[2 * g : 2 * g + 2].reshape(256, NJ)
            t = lax.dot_general(
                zr[g, i].reshape(128, NJ), block, (((1,), (1,)), ((), ())), preferred_element_type=F32
            ).reshape(NP, 16, 256)
            a0 = jnp.sum(jnp.where(mask0[None], t, 0.0), axis=1)
            a1 = jnp.sum(jnp.where(mask1[None], t, 0.0), axis=1)
            rg = a0 + jnp.where(lane8 == 0, -pltpu.roll(a1, 256 - S, 1), pltpu.roll(a1, S, 1))
            for k in range(NP):
                rgp[k, pl.ds(i, 1), g * 256 : (g + 1) * 256] = rg[k : k + 1]
        return c

    lax.fori_loop(0, NI, receivers, 0)

    for g in range(NG):
        part = jnp.dot(bb[g], zr[g].reshape(1024, NJ), preferred_element_type=F32)
        w[2 * g : 2 * g + 2] = part.reshape(2, 128, NJ)

    right = p * NZ + (z + 1) % NZ
    left = p * NZ + (z + NZ - 1) % NZ
    remote(w.at[(z + 4) % NZ], rbuf.at[0], r_send.at[0], r_recv.at[0], right, q).start()
    remote(w.at[(z + 5) % NZ], lbuf.at[0], l_send.at[0], l_recv.at[0], left, q).start()
    for k in range(NP):
        own = jnp.logical_and(k == 0, p // 2 == q)

        @pl.when(jnp.logical_not(own))
        def _():
            remote(rgp.at[k], rgr.at[q, p % 2], g_send.at[k], g_recv.at[q, p % 2], plane(k), p // 2).start()

        @pl.when(own)
        def _():
            pltpu.make_async_copy(rgp.at[k], rgr.at[q, p % 2], g_recv.at[q, p % 2]).start()

    for s in range(1, 4):
        wait_bytes(rbuf.at[s - 1], r_recv.at[s - 1])
        rbuf[s - 1] = rbuf[s - 1] + w[(z + 4 - s) % NZ]
        remote(rbuf.at[s - 1], rbuf.at[s], r_send.at[s], r_recv.at[s], right, q).start()
        if s < 3:
            wait_bytes(lbuf.at[s - 1], l_recv.at[s - 1])
            lbuf[s - 1] = lbuf[s - 1] + w[(z + 5 + s) % NZ]
            remote(lbuf.at[s - 1], lbuf.at[s], l_send.at[s], l_recv.at[s], left, q).start()

    for half in range(2):
        for qq in range(4):
            wait_bytes(rgr.at[qq, half], g_recv.at[qq, half])
        total = (rgr[0, half] + rgr[1, half]) + (rgr[2, half] + rgr[3, half])
        keep = seg_lane[:, 0:1024] < rcounts
        rg_out[:, half * 1024 : (half + 1) * 1024] = jnp.where(keep, total, 0.0)

    wait_bytes(rbuf.at[3], r_recv.at[3])
    wait_bytes(lbuf.at[2], l_recv.at[2])
    done = jnp.where(row_mask, w[z] + rbuf[3] + lbuf[2], 0.0)
    wg_out[...] = lax.dot_general(
        done, onehot, (((1,), (1,)), ((), ())),
        precision=lax.Precision.HIGHEST, preferred_element_type=F32,
    )

    for half in range(2):
        for qq in range(4):
            own = jnp.logical_and((2 * q + half) * NZ + z == r, qq == q)

            @pl.when(jnp.logical_not(own))
            def _():
                wait_bytes(um.at[half], u_send.at[half, qq])

    for k in range(1, NZ):
        wait_bytes(vg.at[z], v_send.at[k])
    for i in range(NI):
        wait_bytes(xs.at[i, 1:NP], x_send.at[i])
        wait_bytes(zs.at[i, 1:NP], z_send.at[i])
    for k in range(NP):
        own = jnp.logical_and(k == 0, p // 2 == q)

        @pl.when(jnp.logical_not(own))
        def _():
            wait_bytes(rgp.at[k], g_send.at[k])

    for s in range(4):
        wait_bytes(rbuf.at[s], r_send.at[s])
    for s in range(3):
        wait_bytes(lbuf.at[s], l_send.at[s])


def shards(receiver_spectra, reference_spectra, receiver_counts, reference_counts, column_station, lag_window, observed):
    table = lag_table()
    m = jnp.asarray(table, dtype=BF)
    mt = jnp.asarray(np.ascontiguousarray(table.T), dtype=BF)
    vmem = pl.BlockSpec(memory_space=pltpu.VMEM)
    dma = pltpu.SemaphoreType.DMA
    return pl.pallas_call(
        kernel,
        out_shape=(
            jax.ShapeDtypeStruct((NI, 2048), F32),
            jax.ShapeDtypeStruct((128, NJ), F32),
        ),
        in_specs=[vmem] * 9,
        out_specs=(vmem, vmem),
        scratch_shapes=[
            pltpu.VMEM((2, NI, 1152), BF),
            pltpu.VMEM((NP, NI, 1152), BF),
            pltpu.VMEM((NZ, 128, NJ), BF),
            pltpu.VMEM((NG, NI, 128, 256), BF),
            pltpu.VMEM((NG, 256, 1024), BF),
            pltpu.VMEM((NP, NI, NJ), F32),
            pltpu.VMEM((NI, NJ), F32),
            pltpu.VMEM((NI, L, NJ), BF),
            pltpu.VMEM((NI, NP, 64, NJ), BF),
            pltpu.VMEM((NI, NP, 64, NJ), BF),
            pltpu.VMEM((2 * L, NJ), BF),
            pltpu.VMEM((NI, NP, NG, 16, NJ), BF),
            pltpu.VMEM((NG, NI, NP, 16, NJ), BF),
            pltpu.VMEM((NZ, 128, NJ), F32),
            pltpu.VMEM((4, 128, NJ), F32),
            pltpu.VMEM((3, 128, NJ), F32),
            pltpu.VMEM((NP, NI, 1024), F32),
            pltpu.VMEM((4, 2, NI, 1024), F32),
            dma((2, 4)), dma((NP,)), dma((NZ,)), dma((NZ,)),
            dma((NI,)), dma((NI,)), dma((NI,)), dma((NI,)),
            dma((NP,)), dma((4, 2)), dma((4,)), dma((4,)), dma((3,)), dma((3,)), dma((1,)),
        ],
        compiler_params=pltpu.CompilerParams(
            collective_id=0, has_side_effects=True, vmem_limit_bytes=60 * 1024 * 1024
        ),
    )(
        receiver_spectra,
        reference_spectra,
        receiver_counts.reshape(NI, 1),
        reference_counts.reshape(1, NJ),
        column_station.reshape(1, NJ),
        lag_window,
        observed,
        m,
        mt,
    )


def solution(mesh):
    return jax.shard_map(
        shards,
        mesh=mesh,
        in_specs=(
            P("rcv", "ref"), P("rcv", "ref"), P("rcv"), P("ref"), P("ref"),
            P(None, "rcv", "ref"), P("rcv", "ref", None),
        ),
        out_specs=(P("rcv", "ref"), P("rcv", "ref")),
        check_vma=False,
    )
```

time: 269 us -> 97.6 us (0.36)
  the two profiles are of different devices: /device:TPU:34 before, /device:TPU:64 now
where the time goes in v1:
time: 97.6 us; the launch traced here: 97.5 us
  Pallas kernels  92.5 us (95%)
  local copies, waits for them, and re-layouts  4.36 us (4%)
    pallas_call x1, Pallas kernels, shards(): pl.pallas_call(kernel, out_shape=(jax.ShapeDtypeStruct((NI, 2048), F32),...  92.5 us
    unnamed x2, local copies, waits for them, and re-layouts  3.04 us

profile of v1, /device:TPU:64, one launch (start us, length us, event | category | flops | bytes accessed | tf_op | source)
XLA Modules:
  0.0 97.5 jit_solution(4664656026033028856)
XLA Ops:
  0.6 1.3 %copy.11.rc_ref = s32[8,1]{1,0:T(8,128)} copy(s32[8,1]{0,1:T(1,128)} %bitcast.5) | data formatting | bytes 64 | tf_op jit(solution)/shard_map/reshape | solution.py:345
  2.0 92.5 %shard_map.104 = (f32[8,2048]{1,0:T(8,128)}, f32[128,256]{1,0:T(8,128)}) custom-call(bf16[8,2048]{1,0:T(8,128)(2,1)} %u_ref.1, bf16[128,256]{1,0:T(8,128)(2,1)} %v_ref.1, s32[8,1]{1,0:T(8,128)} %copy.11.rc_ref, s32[1,256]{1,0:T(1,128)} %bitcast.3, s32[1,256]{1,0:T(1,128)} %bitcast.4, s32[2,8,256]{2,1,0:T(8,128)} %win_ref.1, bf16[8,256,512]{2,1,0:T(8,128)(2,1)} %obs_ref.1, ...), custom_call_target="tpu_custom_call" | custom-call | tf_op jit(solution)/shard_map/pallas_call | solution.py:308
  94.4 1.5 %copy.14 = f32[8,2048]{1,0:T(8,128)} copy(f32[8,2048]{1,0:T(8,128)} %get-tuple-element.4) | data formatting | bytes 131072
  95.9 1.6 %copy.15 = f32[128,256]{1,0:T(8,128)} copy(f32[128,256]{1,0:T(8,128)} %get-tuple-element.5) | data formatting | bytes 262144

commit v2 on v1

v2 whole, which is shorter than its diff:
```python
import math

import jax
import jax.numpy as jnp
import numpy as np
from jax import lax
from jax.experimental import pallas as pl
from jax.experimental.pallas import tpu as pltpu
from jax.sharding import PartitionSpec as P

L = 512
S = 16
F = 256
NP = 8
NZ = 8
NI = 8
NJ = 256
NG = 4
MESH = pl.DeviceIdType.MESH
BF = jnp.bfloat16
F32 = jnp.float32

env_floor = 0.05
misfit_scale = 0.03125


def lag_table():
    freq_ids = np.arange(F, dtype=np.int64)[:, None]
    lag_ids = np.arange(L, dtype=np.int64)[None, :] - L // 2
    angle = ((freq_ids * lag_ids) % L).astype(np.float64) * (2.0 * math.pi / L)
    cosine = np.cos(angle) / math.sqrt(F)
    sine = np.sin(angle) / math.sqrt(F)
    real_rows = np.concatenate([cosine, sine], axis=1)
    imag_rows = np.concatenate([-sine, cosine], axis=1)
    stacked = np.stack([real_rows, imag_rows], axis=1).reshape(2 * F, 2 * L)
    return stacked.astype(np.float32)


def kernel(
    u_ref, v_ref, rc_ref, fc_ref, cs_ref, win_ref, obs_hbm, m_hbm, mt_hbm,
    rg_out, wg_out,
    um, us, vg, bt, bb, rinv, ninv, first, last, obs, m_ref, mt_ref, obst, xs, xr, gs, zs, zr,
    w, rbuf, lbuf, rgp, rgr,
    in_sem, u_send, u_recv, v_send, v_recv, x_send, x_recv, z_send, z_recv,
    g_send, g_recv, r_send, r_recv, l_send, l_recv,
):
    r = lax.axis_index("rcv")
    q = lax.axis_index("ref")
    p = r // NZ
    z = r % NZ

    def signal(rr, qq):
        pl.semaphore_signal(barrier, inc=1, device_id=(rr, qq), device_id_type=MESH)

    def remote(src, dst, send, recv, rr, qq):
        return pltpu.make_async_remote_copy(
            src_ref=src, dst_ref=dst, send_sem=send, recv_sem=recv,
            device_id=(rr, qq), device_id_type=MESH,
        )

    def plane(k):
        return ((p + k) % NP) * NZ + z

    def wait_bytes(ref, sem):
        pltpu.make_async_copy(ref, ref, sem).wait()

    barrier = pltpu.get_barrier_semaphore()
    for k in range(1, NP):
        signal(plane(k), q)
    for k in range(1, NZ):
        signal(p * NZ + (z + k) % NZ, q)
    for k in range(NP):
        own = jnp.logical_and(k == 0, p // 2 == q)

        @pl.when(jnp.logical_not(own))
        def _():
            signal(plane(k), p // 2)

    for half in range(2):
        for qq in range(4):
            rr = (2 * q + half) * NZ + z
            own = jnp.logical_and(rr == r, qq == q)

            @pl.when(jnp.logical_not(own))
            def _():
                signal(rr, qq)

    loads = [pltpu.make_async_copy(obs_hbm.at[i], obs.at[i], in_sem.at[i]) for i in range(NI)]
    loads.append(pltpu.make_async_copy(mt_hbm, mt_ref, in_sem.at[NI]))
    loads.append(pltpu.make_async_copy(m_hbm, m_ref, in_sem.at[NI + 1]))
    for load in loads:
        load.start()

    eye = lax.broadcasted_iota(jnp.int32, (NI, NI), 0) == lax.broadcasted_iota(jnp.int32, (NI, NI), 1)
    rcounts = jnp.sum(jnp.where(eye, rc_ref[...].astype(F32), 0.0), axis=1, keepdims=True)
    pc = fc_ref[...].astype(F32)
    row_mask = (lax.broadcasted_iota(jnp.int32, (128, NJ), 0) % S).astype(F32) < pc
    mine = jnp.where(row_mask, v_ref[...].astype(F32), 0.0).astype(BF)
    for h in range(2):
        vg[h, z] = mine[:, h * 128 : (h + 1) * 128]
    seg_lane = (lax.broadcasted_iota(jnp.int32, (NI, 1024), 1) % S).astype(F32)
    keep = seg_lane < rcounts
    for half in range(2):
        part = u_ref[:, half * 1024 : (half + 1) * 1024].astype(F32)
        um[half, :, 0:1024] = jnp.where(keep, part, 0.0).astype(BF)
        um[half, :, 1024:1152] = jnp.broadcast_to(rcounts, (NI, 128)).astype(BF)

    order = cs_ref[...] - q * NJ
    stations = lax.broadcasted_iota(jnp.int32, (NJ, NJ), 0)
    onehot = jnp.where(stations == order, 1.0, 0.0).astype(BF)
    nt = (((1,), (1,)), ((), ()))
    begin = lax.dot_general(win_ref[0].astype(F32).astype(BF), onehot, nt, preferred_element_type=F32)
    span = lax.dot_general(win_ref[1].astype(F32).astype(BF), onehot, nt, preferred_element_type=F32)
    inv = 1.0 / jnp.minimum(rcounts, pc)
    for h in range(2):
        for i in range(NI):
            u, lanes, side = 4 * h + i // 2, pl.ds((i % 2) * 128, 128), slice(h * 128, (h + 1) * 128)
            first[u : u + 1, lanes] = begin[i : i + 1, side]
            last[u : u + 1, lanes] = begin[i : i + 1, side] + span[i : i + 1, side]
            ninv[u : u + 1, lanes] = inv[i : i + 1, side]
    for i in range(NI):
        loads[i].wait()

    def turn(ii, c):
        for par in range(2):
            seen = jnp.dot(onehot, obs[2 * ii + par], preferred_element_type=F32)
            seen = jnp.transpose(seen, (1, 0)).astype(BF)
            for h in range(2):
                obst[4 * h + ii, :, par * 128 : (par + 1) * 128] = seen[:, h * 128 : (h + 1) * 128]
        return c

    lax.fori_loop(0, NI // 2, turn, 0)

    pl.semaphore_wait(barrier, 2 * (NP - 1) + 2 * NP - jnp.where(p // 2 == q, 2, 0))

    for half in range(2):
        for qq in range(4):
            pp = 2 * q + half
            rr = pp * NZ + z
            own = jnp.logical_and(rr == r, qq == q)
            slot = (p - pp + NP) % NP

            @pl.when(jnp.logical_not(own))
            def _():
                remote(um.at[half], us.at[slot], u_send.at[half, qq], u_recv.at[slot], rr, qq).start()

            @pl.when(own)
            def _():
                pltpu.make_async_copy(um.at[half], us.at[slot], u_recv.at[slot]).start()

    for h in range(2):
        for k in (1, 7, 2, 6, 3, 5, 4):
            remote(
                vg.at[h, z], vg.at[h, z], v_send.at[h], v_recv.at[h, z], p * NZ + (z + k) % NZ, q
            ).start()

    row16 = lax.broadcasted_iota(jnp.int32, (16, 256), 0)
    lane256 = lax.broadcasted_iota(jnp.int32, (16, 256), 1)
    diag = (lane256 // 32) == (row16 // 2)
    mask0 = jnp.logical_and(diag, row16 % 2 == 0)
    mask1 = jnp.logical_and(diag, row16 % 2 == 1)

    def operand(k, c):
        wait_bytes(us.at[k], u_recv.at[k])
        uf = us[k, :, 0:1024].astype(F32)
        part = (lax.broadcasted_iota(jnp.int32, (NI, 1024), 1) // S) % 2
        turned = jnp.where(part == 0, pltpu.roll(uf, 1024 - S, 1), -pltpu.roll(uf, S, 1))
        inverse = 1.0 / jnp.minimum(us[k, :, 1024:1025].astype(F32), pc)
        for h in range(2):
            rinv[h, k] = inverse[:, h * 128 : (h + 1) * 128]
        for g in range(NG):
            a = uf[:, g * 256 : (g + 1) * 256]
            b = turned[:, g * 256 : (g + 1) * 256]
            for i in range(NI):
                blk = jnp.where(mask0, a[i : i + 1], jnp.where(mask1, b[i : i + 1], 0.0))
                bt[g, i // 2, i % 2, pl.ds(k * 16, 16), :] = blk.astype(BF)
        return c

    lax.fori_loop(0, NP, operand, 0)

    for h in range(2):
        for k in range(1, NZ):
            zz = (z + k) % NZ
            wait_bytes(vg.at[h, zz], v_recv.at[h, zz])

        def cross(ii, c):
            u = 4 * h + ii
            scale = jnp.concatenate(
                [
                    jnp.broadcast_to(rinv[h, k, pl.ds(2 * ii + par, 1), :], (16, 128))
                    for par in range(2)
                    for k in range(NP)
                ],
                axis=0,
            )
            for g in range(NG):
                block = vg[h, 2 * g : 2 * g + 2].reshape(256, 128)
                x = jnp.dot(bt[g, ii].reshape(256, 256), block, preferred_element_type=F32) * scale
                x = x.astype(BF)
                for par in range(2):
                    lanes = slice(par * 128, (par + 1) * 128)
                    rows = slice(g * 16, (g + 1) * 16)
                    xr[u, p, rows, lanes] = x[par * 128 : par * 128 + 16]
                    for k in range(1, NP):
                        xs[u, k, rows, lanes] = x[par * 128 + k * 16 : par * 128 + (k + 1) * 16]
            for k in range(1, NP):
                remote(xs.at[u, k], xr.at[u, p], x_send.at[u], x_recv.at[u], plane(k), q).start()
            return c

        lax.fori_loop(0, 4, cross, 0)

    def flip(g, c):
        for ii in range(4):
            for par in range(2):
                bb[g, par, :, ii * 128 : (ii + 1) * 128] = jnp.transpose(
                    bt[g, ii, par].astype(F32), (1, 0)
                ).astype(BF)
        return c

    lax.fori_loop(0, NG, flip, 0)

    TB = 128
    loads[NI].wait()
    loads[NI + 1].wait()

    def pairs(u, c):
        wait_bytes(xs.at[u, 1:NP], x_recv.at[u])
        x = xr[u].reshape(2 * F, NJ)
        lo = first[pl.ds(u, 1), :]
        hi = last[pl.ds(u, 1), :]
        for b in range(L // TB):
            cor = jnp.dot(mt_ref[b * TB : (b + 1) * TB, :], x, preferred_element_type=F32)
            hil = jnp.dot(mt_ref[L + b * TB : L + (b + 1) * TB, :], x, preferred_element_type=F32)
            rs = lax.rsqrt(cor * cor + hil * hil + env_floor)
            lag = (lax.broadcasted_iota(jnp.int32, (TB, NJ), 0) + b * TB).astype(F32)
            inside = jnp.logical_and(lag >= lo, lag < hi)
            seen = obst[u, b * TB : (b + 1) * TB, :].astype(F32)
            wt = jnp.where(inside, (1.0 - seen * rs) * misfit_scale, 0.0)
            gs[b * TB : (b + 1) * TB, :] = (wt * cor).astype(BF)
            gs[L + b * TB : L + (b + 1) * TB, :] = (wt * hil).astype(BF)
        scale = ninv[pl.ds(u, 1), :]
        for b in range(4):
            back = jnp.dot(m_ref[b * 128 : (b + 1) * 128, :], gs[...], preferred_element_type=F32)
            zs[u, 2 * b : 2 * b + 2] = (back * scale).astype(BF).reshape(2, NG, 16, NJ)
        for k in range(1, NP):
            remote(
                zs.at[u, (p + k) % NP], zr.at[:, u, NP - k], z_send.at[u], z_recv.at[u], plane(k), q
            ).start()
        zr[:, u, 0] = zs[u, p]
        return c

    lax.fori_loop(0, 8, pairs, 0)

    right = p * NZ + (z + 1) % NZ
    left = p * NZ + (z + NZ - 1) % NZ

    def arrived(u):
        wait_bytes(zs.at[u, 1:NP], z_recv.at[u])

    def sums(h):
        for g in range(NG):
            part = jnp.dot(
                bb[g, 0], zr[g, 4 * h : 4 * h + 4, :, :, 0:128].reshape(512, 128), preferred_element_type=F32
            ) + jnp.dot(
                bb[g, 1], zr[g, 4 * h : 4 * h + 4, :, :, 128:256].reshape(512, 128), preferred_element_type=F32
            )
            w[h, 2 * g : 2 * g + 2] = part.reshape(2, 128, 128)

    def ring(h, s):
        for n in range(2):
            rows = slice(n * 64, (n + 1) * 64)
            if s > 0:
                wait_bytes(rbuf.at[h, s - 1, rows], r_recv.at[h, s - 1, n])
                rbuf[h, s - 1, rows] = rbuf[h, s - 1, rows] + w[h, (z + 4 - s) % NZ, rows]
            src = rbuf.at[h, s - 1, rows] if s > 0 else w.at[h, (z + 4) % NZ, rows]
            remote(src, rbuf.at[h, s, rows], r_send.at[h, s, n], r_recv.at[h, s, n], right, q).start()
            if s > 2:
                continue
            if s > 0:
                wait_bytes(lbuf.at[h, s - 1, rows], l_recv.at[h, s - 1, n])
                lbuf[h, s - 1, rows] = lbuf[h, s - 1, rows] + w[h, (z + 5 + s) % NZ, rows]
            src = lbuf.at[h, s - 1, rows] if s > 0 else w.at[h, (z + 5) % NZ, rows]
            remote(src, lbuf.at[h, s, rows], l_send.at[h, s, n], l_recv.at[h, s, n], left, q).start()

    def ring_end(h):
        for n in range(2):
            rows = slice(n * 64, (n + 1) * 64)
            wait_bytes(rbuf.at[h, 3, rows], r_recv.at[h, 3, n])
            wait_bytes(lbuf.at[h, 2, rows], l_recv.at[h, 2, n])
            keep = row_mask[rows, h * 128 : (h + 1) * 128]
            done = w[h, z, rows] + rbuf[h, 3, rows] + lbuf[h, 2, rows]
            wg_out[rows, h * 128 : (h + 1) * 128] = jnp.where(keep, done, 0.0)

    lane8 = (lax.broadcasted_iota(jnp.int32, (NP, 256), 1) // S) % 2

    def receivers(ii):
        for g in range(NG):
            for par in range(2):
                t = None
                for h in range(2):
                    got = zr[g, 4 * h + ii, :, :, par * 128 : (par + 1) * 128].reshape(128, 128)
                    block = vg[h, 2 * g : 2 * g + 2].reshape(256, 128)
                    part = lax.dot_general(got, block, nt, preferred_element_type=F32)
                    t = part if t is None else t + part
                t = t.reshape(NP, 16, 256)
                a0 = jnp.sum(jnp.where(mask0[None], t, 0.0), axis=1)
                a1 = jnp.sum(jnp.where(mask1[None], t, 0.0), axis=1)
                rg = a0 + jnp.where(lane8 == 0, -pltpu.roll(a1, 256 - S, 1), pltpu.roll(a1, S, 1))
                i = 2 * ii + par
                for k in range(NP):
                    rgp[k, i : i + 1, g * 256 : (g + 1) * 256] = rg[k : k + 1]

    for u in range(4):
        arrived(u)
    sums(0)
    ring(0, 0)
    for s in range(1, 4):
        arrived(3 + s)
        receivers(s - 1)
        ring(0, s)
    arrived(7)
    sums(1)
    ring(1, 0)
    receivers(3)
    for k in range(NP):
        own = jnp.logical_and(k == 0, p // 2 == q)

        @pl.when(jnp.logical_not(own))
        def _():
            remote(rgp.at[k], rgr.at[q, p % 2], g_send.at[k], g_recv.at[q, p % 2], plane(k), p // 2).start()

        @pl.when(own)
        def _():
            pltpu.make_async_copy(rgp.at[k], rgr.at[q, p % 2], g_recv.at[q, p % 2]).start()

    ring(1, 1)
    ring_end(0)
    ring(1, 2)
    ring(1, 3)
    for half in range(2):
        for qq in range(4):
            wait_bytes(rgr.at[qq, half], g_recv.at[qq, half])
        total = (rgr[0, half] + rgr[1, half]) + (rgr[2, half] + rgr[3, half])
        rg_out[:, half * 1024 : (half + 1) * 1024] = jnp.where(keep, total, 0.0)
    ring_end(1)

    for half in range(2):
        for qq in range(4):
            own = jnp.logical_and((2 * q + half) * NZ + z == r, qq == q)

            @pl.when(jnp.logical_not(own))
            def _():
                wait_bytes(um.at[half], u_send.at[half, qq])

    for h in range(2):
        wait_bytes(vg.at[h, 1:NZ], v_send.at[h])
    for u in range(8):
        wait_bytes(xs.at[u, 1:NP], x_send.at[u])
        wait_bytes(zs.at[u, 1:NP], z_send.at[u])
    for k in range(NP):
        own = jnp.logical_and(k == 0, p // 2 == q)

        @pl.when(jnp.logical_not(own))
        def _():
            wait_bytes(rgp.at[k], g_send.at[k])

    for h in range(2):
        for n in range(2):
            rows = slice(n * 64, (n + 1) * 64)
            for s in range(4):
                wait_bytes(rbuf.at[h, s, rows], r_send.at[h, s, n])
            for s in range(3):
                wait_bytes(lbuf.at[h, s, rows], l_send.at[h, s, n])


def shards(receiver_spectra, reference_spectra, receiver_counts, reference_counts, column_station, lag_window, observed):
    table = lag_table()
    m = jnp.asarray(table, dtype=BF)
    mt = jnp.asarray(np.ascontiguousarray(table.T), dtype=BF)
    vmem = pl.BlockSpec(memory_space=pltpu.VMEM)
    hbm = pl.BlockSpec(memory_space=pl.ANY)
    dma = pltpu.SemaphoreType.DMA
    return pl.pallas_call(
        kernel,
        out_shape=(
            jax.ShapeDtypeStruct((NI, 2048), F32),
            jax.ShapeDtypeStruct((128, NJ), F32),
        ),
        in_specs=[vmem] * 6 + [hbm] * 3,
        out_specs=(vmem, vmem),
        scratch_shapes=[
            pltpu.VMEM((2, NI, 1152), BF),
            pltpu.VMEM((NP, NI, 1152), BF),
            pltpu.VMEM((2, NZ, 128, 128), BF),
            pltpu.VMEM((NG, 4, 2, 128, 256), BF),
            pltpu.VMEM((NG, 2, 256, 512), BF),
            pltpu.VMEM((2, NP, NI, 128), F32),
            pltpu.VMEM((8, NJ), F32),
            pltpu.VMEM((8, NJ), F32),
            pltpu.VMEM((8, NJ), F32),
            pltpu.VMEM((NI, NJ, L), BF),
            pltpu.VMEM((2 * F, 2 * L), BF),
            pltpu.VMEM((2 * L, 2 * F), BF),
            pltpu.VMEM((8, L, NJ), BF),
            pltpu.VMEM((8, NP, 64, NJ), BF),
            pltpu.VMEM((8, NP, 64, NJ), BF),
            pltpu.VMEM((2 * L, NJ), BF),
            pltpu.VMEM((8, NP, NG, 16, NJ), BF),
            pltpu.VMEM((NG, 8, NP, 16, NJ), BF),
            pltpu.VMEM((2, NZ, 128, 128), F32),
            pltpu.VMEM((2, 4, 128, 128), F32),
            pltpu.VMEM((2, 3, 128, 128), F32),
            pltpu.VMEM((NP, NI, 1024), F32),
            pltpu.VMEM((4, 2, NI, 1024), F32),
            dma((NI + 2,)), dma((2, 4)), dma((NP,)), dma((2,)), dma((2, NZ)),
            dma((8,)), dma((8,)), dma((8,)), dma((8,)),
            dma((NP,)), dma((4, 2)), dma((2, 4, 2)), dma((2, 4, 2)), dma((2, 3, 2)), dma((2, 3, 2)),
        ],
        compiler_params=pltpu.CompilerParams(
            collective_id=0, has_side_effects=True, vmem_limit_bytes=60 * 1024 * 1024
        ),
    )(
        receiver_spectra,
        reference_spectra,
        receiver_counts.reshape(1, NI),
        reference_counts.reshape(1, NJ),
        column_station.reshape(1, NJ),
        lag_window,
        observed,
        m,
        mt,
    )


def solution(mesh):
    return jax.shard_map(
        shards,
        mesh=mesh,
        in_specs=(
            P("rcv", "ref"), P("rcv", "ref"), P("rcv"), P("ref"), P("ref"),
            P(None, "rcv", "ref"), P("rcv", "ref", None),
        ),
        out_specs=(P("rcv", "ref"), P("rcv", "ref")),
        check_vma=False,
    )
```

time: 97.6 us -> 89.9 us (0.921)
  the two profiles are of different devices: /device:TPU:64 before, /device:TPU:2 now
where the time goes in v2:
time: 89.9 us; the launch traced here: 89.2 us
  Pallas kernels  85.5 us (95%)
  local copies, waits for them, and re-layouts  3.04 us (3%)
    pallas_call x1, Pallas kernels, shards(): pl.pallas_call(kernel, out_shape=(jax.ShapeDtypeStruct((NI, 2048), F32),...  85.5 us
    unnamed x2, local copies, waits for them, and re-layouts  3.04 us

profile of v2, /device:TPU:2, one launch (start us, length us, event | category | flops | bytes accessed | tf_op | source)
XLA Modules:
  0.0 89.2 jit_solution(8020867411138616332)
XLA Ops:
  0.6 85.5 %shard_map.104 = (f32[8,2048]{1,0:T(8,128)}, f32[128,256]{1,0:T(8,128)}) custom-call(bf16[8,2048]{1,0:T(8,128)(2,1)} %u_ref.1, bf16[128,256]{1,0:T(8,128)(2,1)} %v_ref.1, s32[1,8]{1,0:T(1,128)} %bitcast.5, s32[1,256]{1,0:T(1,128)} %bitcast.3, s32[1,256]{1,0:T(1,128)} %bitcast.4, s32[2,8,256]{2,1,0:T(8,128)} %win_ref.1, bf16[8,256,512]{2,1,0:T(8,128)(2,1)} %obs_hbm.1, ...), custom_call_target="tpu_custom_call" | custom-call | tf_op jit(solution)/shard_map/pallas_call | solution.py:383
  86.2 1.5 %copy.13 = f32[8,2048]{1,0:T(8,128)} copy(f32[8,2048]{1,0:T(8,128)} %get-tuple-element.4) | data formatting | bytes 131072
  87.6 1.6 %copy.14 = f32[128,256]{1,0:T(8,128)} copy(f32[128,256]{1,0:T(8,128)} %get-tuple-element.5) | data formatting | bytes 262144

commit v3 on v2

--- a/solution.py
+++ b/solution.py
@@ -383,11 +383,11 @@
     return pl.pallas_call(
         kernel,
         out_shape=(
-            jax.ShapeDtypeStruct((NI, 2048), F32),
-            jax.ShapeDtypeStruct((128, NJ), F32),
+            pltpu.VMEM((NI, 2048), F32),
+            pltpu.VMEM((128, NJ), F32),
         ),
         in_specs=[vmem] * 6 + [hbm] * 3,
-        out_specs=(vmem, vmem),
+        out_specs=(pl.BlockSpec(memory_space=pltpu.MemorySpace.VMEM), pl.BlockSpec(memory_space=pltpu.MemorySpace.VMEM)),
         scratch_shapes=[
             pltpu.VMEM((2, NI, 1152), BF),
             pltpu.VMEM((NP, NI, 1152), BF),

time: 89.9 us -> 87.5 us (0.973)
  local copies, waits for them, and re-layouts: 3.04 us -> 1.29 us
    unnamed x2, local copies, waits for them, and re-layouts: 3.04 us -> 1.29 us
where the time goes in v3:
time: 87.5 us; the launch traced here: 86.8 us
  Pallas kernels  84.8 us (97%)
  local copies, waits for them, and re-layouts  1.29 us (1%)
    pallas_call x1, Pallas kernels, shards(): pl.pallas_call(kernel, out_shape=(pltpu.VMEM((NI, 2048), F32), pltpu.VMEM...  84.8 us

profile of v3, /device:TPU:2, one launch (start us, length us, event | category | flops | bytes accessed | tf_op | source)
XLA Modules:
  0.0 86.8 jit_solution(4067982638640368152)
XLA Ops:
  0.6 84.8 %shard_map.104 = (f32[8,2048]{1,0:T(8,128)S(1)}, f32[128,256]{1,0:T(8,128)S(1)}) custom-call(bf16[8,2048]{1,0:T(8,128)(2,1)} %u_ref.1, bf16[128,256]{1,0:T(8,128)(2,1)} %v_ref.1, s32[1,8]{1,0:T(1,128)} %bitcast.5, s32[1,256]{1,0:T(1,128)} %bitcast.3, s32[1,256]{1,0:T(1,128)} %bitcast.4, s32[2,8,256]{2,1,0:T(8,128)} %win_ref.1, bf16[8,256,512]{2,1,0:T(8,128)(2,1)} %obs_hbm.1, ...), custom_call_target="tpu_custom_call" | custom-call | tf_op jit(solution)/shard_map/pallas_call | solution.py:383
  85.5 0.6 copy.13
  86.1 0.7 copy.14

commit v4 on v3

--- a/solution.py
+++ b/solution.py
@@ -37,17 +37,25 @@
 
 
 def kernel(
-    u_ref, v_ref, rc_ref, fc_ref, cs_ref, win_ref, obs_hbm, m_hbm, mt_hbm,
+    u_ref, v_ref, rc_ref, fc_ref, cs_ref, win_ref, obs_hbm, m_hbm, mq_hbm, mr_hbm,
     rg_out, wg_out,
-    um, us, vg, bt, bb, rinv, ninv, first, last, obs, m_ref, mt_ref, obst, xs, xr, gs, zs, zr,
+    um, us, ur, uq, vr, vq, ucr, ucq, bw, scr, scq, bt, bb, ninv, first, last,
+    obs, m_ref, mq_ref, mr_ref, obst, xsr, xrr, xsq, xrq, gs, zs, zr,
     w, rbuf, lbuf, rgp, rgr,
-    in_sem, u_send, u_recv, v_send, v_recv, x_send, x_recv, z_send, z_recv,
+    in_sem, u_send, u_recv, ur_send, ur_recv, uq_send, uq_recv,
+    vx_send, vx_recv, vy_send, vy_recv, vr_send, vr_recv, vq_send, vq_recv,
+    xr_send, xr_recv, xq_send, xq_recv, z_send, z_recv,
     g_send, g_recv, r_send, r_recv, l_send, l_recv,
 ):
     r = lax.axis_index("rcv")
     q = lax.axis_index("ref")
     p = r // NZ
     z = r % NZ
+    x = p // 4
+    y = p % 4
+    right = p * NZ + (z + 1) % NZ
+    left = p * NZ + (z + NZ - 1) % NZ
+    partner = ((p + 4) % NP) * NZ + z
 
     def signal(rr, qq):
         pl.semaphore_signal(barrier, inc=1, device_id=(rr, qq), device_id_type=MESH)
@@ -65,29 +73,17 @@
         pltpu.make_async_copy(ref, ref, sem).wait()
 
     barrier = pltpu.get_barrier_semaphore()
-    for k in range(1, NP):
-        signal(plane(k), q)
-    for k in range(1, NZ):
-        signal(p * NZ + (z + k) % NZ, q)
     for k in range(NP):
-        own = jnp.logical_and(k == 0, p // 2 == q)
-
-        @pl.when(jnp.logical_not(own))
-        def _():
-            signal(plane(k), p // 2)
-
-    for half in range(2):
-        for qq in range(4):
-            rr = (2 * q + half) * NZ + z
-            own = jnp.logical_and(rr == r, qq == q)
-
-            @pl.when(jnp.logical_not(own))
-            def _():
-                signal(rr, qq)
+        for dq in range(4):
+            if k or dq:
+                signal(plane(k), (q + dq) % 4)
+    signal(right, q)
+    signal(left, q)
 
     loads = [pltpu.make_async_copy(obs_hbm.at[i], obs.at[i], in_sem.at[i]) for i in range(NI)]
-    loads.append(pltpu.make_async_copy(mt_hbm, mt_ref, in_sem.at[NI]))
+    loads.append(pltpu.make_async_copy(mr_hbm, mr_ref, in_sem.at[NI]))
     loads.append(pltpu.make_async_copy(m_hbm, m_ref, in_sem.at[NI + 1]))
+    loads.append(pltpu.make_async_copy(mq_hbm, mq_ref, in_sem.at[NI + 2]))
     for load in loads:
         load.start()
 
@@ -96,8 +92,8 @@
     pc = fc_ref[...].astype(F32)
     row_mask = (lax.broadcasted_iota(jnp.int32, (128, NJ), 0) % S).astype(F32) < pc
     mine = jnp.where(row_mask, v_ref[...].astype(F32), 0.0).astype(BF)
-    for h in range(2):
-        vg[h, z] = mine[:, h * 128 : (h + 1) * 128]
+    vq[z, y] = mine[:, 0:128]
+    vr[z, x] = mine[:, 128:256]
     seg_lane = (lax.broadcasted_iota(jnp.int32, (NI, 1024), 1) % S).astype(F32)
     keep = seg_lane < rcounts
     for half in range(2):
@@ -131,28 +127,92 @@
 
     lax.fori_loop(0, NI // 2, turn, 0)
 
-    pl.semaphore_wait(barrier, 2 * (NP - 1) + 2 * NP - jnp.where(p // 2 == q, 2, 0))
-
+    pl.semaphore_wait(barrier, 4 * NP - 1 + 2)
+
+    def give(own, src, dst, send, recv, rr, qq):
+        @pl.when(jnp.logical_not(own))
+        def _():
+            remote(src, dst, send, recv, rr, qq).start()
+
+        @pl.when(own)
+        def _():
+            pltpu.make_async_copy(src, dst, recv).start()
+
+    def pass_on(buf, send, recv, zz, sub, to):
+        remote(buf.at[zz, sub], buf.at[zz, sub], send.at[0], recv.at[zz, sub], to, q).start()
+
+    def pass_r(zz, sub, to):
+        pass_on(vr, vr_send, vr_recv, zz, sub, to)
+
+    def pass_q(zz, sub, to):
+        pass_on(vq, vq_send, vq_recv, zz, sub, to)
+
+    remote(vr.at[z, x], vr.at[z, x], vx_send.at[0], vx_recv.at[0], partner, q).start()
+    for k in range(1, 4):
+        remote(
+            vq.at[z, y], vq.at[z, y], vy_send.at[0], vy_recv.at[y], (x * 4 + (y + k) % 4) * NZ + z, q
+        ).start()
+    pass_r(z, x, right)
+    pass_r(z, x, left)
+    pass_q(z, y, right)
+    pass_q(z, y, left)
+    for half in range(2):
+        for qq in range(4):
+            yd = 2 * (q % 2) + half
+            own = jnp.logical_and(yd == y, qq == q)
+            give(
+                own, um.at[half], ur.at[(y - yd + 4) % 4, q // 2], ur_send.at[half, qq],
+                ur_recv.at[(y - yd + 4) % 4, q // 2], (x * 4 + yd) * NZ + z, qq,
+            )
+    for qq in range(4):
+        xd = q // 2
+        own = jnp.logical_and(xd == x, qq == q)
+        give(
+            own, um, uq.at[(x - xd + 2) % 2, q % 2], uq_send.at[qq],
+            uq_recv.at[(x - xd + 2) % 2, q % 2], (xd * 4 + y) * NZ + z, qq,
+        )
+    wait_bytes(vr.at[z, 1 - x], vx_recv.at[0])
+    pass_r(z, 1 - x, right)
+    pass_r(z, 1 - x, left)
+    for k in (1, 3, 2):
+        yy = (y + k) % 4
+        wait_bytes(vq.at[z, yy], vy_recv.at[yy])
+        pass_q(z, yy, right)
+        pass_q(z, yy, left)
     for half in range(2):
         for qq in range(4):
             pp = 2 * q + half
             rr = pp * NZ + z
             own = jnp.logical_and(rr == r, qq == q)
             slot = (p - pp + NP) % NP
-
-            @pl.when(jnp.logical_not(own))
-            def _():
-                remote(um.at[half], us.at[slot], u_send.at[half, qq], u_recv.at[slot], rr, qq).start()
-
-            @pl.when(own)
-            def _():
-                pltpu.make_async_copy(um.at[half], us.at[slot], u_recv.at[slot]).start()
-
-    for h in range(2):
-        for k in (1, 7, 2, 6, 3, 5, 4):
-            remote(
-                vg.at[h, z], vg.at[h, z], v_send.at[h], v_recv.at[h, z], p * NZ + (z + k) % NZ, q
-            ).start()
+            give(own, um.at[half], us.at[slot], u_send.at[half, qq], u_recv.at[slot], rr, qq)
+
+    def back(s):
+        return (z + NZ - s) % NZ
+
+    def ahead(s):
+        return (z + s) % NZ
+
+    def step_r(s):
+        for k in range(2):
+            sub = (x + k) % 2
+            if s < 4:
+                wait_bytes(vr.at[back(s), sub], vr_recv.at[back(s), sub])
+                if s < 3:
+                    pass_r(back(s), sub, right)
+            wait_bytes(vr.at[ahead(s), sub], vr_recv.at[ahead(s), sub])
+            if s < 4:
+                pass_r(ahead(s), sub, left)
+
+    def step_q(s):
+        for k in (0, 1, 3, 2):
+            sub = (y + k) % 4
+            wait_bytes(vq.at[back(s), sub], vq_recv.at[back(s), sub])
+            if s < 4:
+                pass_q(back(s), sub, right)
+                wait_bytes(vq.at[ahead(s), sub], vq_recv.at[ahead(s), sub])
+                if s < 3:
+                    pass_q(ahead(s), sub, left)
 
     row16 = lax.broadcasted_iota(jnp.int32, (16, 256), 0)
     lane256 = lax.broadcasted_iota(jnp.int32, (16, 256), 1)
@@ -160,77 +220,120 @@
     mask0 = jnp.logical_and(diag, row16 % 2 == 0)
     mask1 = jnp.logical_and(diag, row16 % 2 == 1)
 
-    def operand(k, c):
-        wait_bytes(us.at[k], u_recv.at[k])
-        uf = us[k, :, 0:1024].astype(F32)
+    def turned(uf):
         part = (lax.broadcasted_iota(jnp.int32, (NI, 1024), 1) // S) % 2
-        turned = jnp.where(part == 0, pltpu.roll(uf, 1024 - S, 1), -pltpu.roll(uf, S, 1))
-        inverse = 1.0 / jnp.minimum(us[k, :, 1024:1025].astype(F32), pc)
-        for h in range(2):
-            rinv[h, k] = inverse[:, h * 128 : (h + 1) * 128]
-        for g in range(NG):
-            a = uf[:, g * 256 : (g + 1) * 256]
-            b = turned[:, g * 256 : (g + 1) * 256]
+        return jnp.where(part == 0, pltpu.roll(uf, 1024 - S, 1), -pltpu.roll(uf, S, 1))
+
+    def blocks(a, b, out):
+        for i in range(NI):
+            out(i, jnp.where(mask0, a[i : i + 1], jnp.where(mask1, b[i : i + 1], 0.0)).astype(BF))
+
+    def ready_r(yk, c):
+        for xx in range(2):
+            wait_bytes(ur.at[yk, xx], ur_recv.at[yk, xx])
+            uf = ur[yk, xx, :, 0:1024].astype(F32)
+            ut = turned(uf)
+            for zz in range(NZ):
+                ucr[zz, yk, 0, :, xx * 128 : (xx + 1) * 128] = uf[:, zz * 128 : (zz + 1) * 128]
+                ucr[zz, yk, 1, :, xx * 128 : (xx + 1) * 128] = ut[:, zz * 128 : (zz + 1) * 128]
+        inverse = 1.0 / jnp.minimum(ur[yk, 0, :, 1024:1025].astype(F32), pc[:, 128:256])
+        for i in range(NI):
+            scr[yk, i] = jnp.broadcast_to(inverse[i : i + 1], (16, 128))
+        return c
+
+    def ready_q(xk, c):
+        for b in range(2):
+            wait_bytes(uq.at[xk, b], uq_recv.at[xk, b])
+            for half in range(2):
+                uf = uq[xk, b, half, :, 0:1024].astype(F32)
+                ut = turned(uf)
+                for zz in range(NZ):
+                    ucq[zz, xk, b, 0, :, half * 128 : (half + 1) * 128] = uf[:, zz * 128 : (zz + 1) * 128]
+                    ucq[zz, xk, b, 1, :, half * 128 : (half + 1) * 128] = ut[:, zz * 128 : (zz + 1) * 128]
+        inverse = 1.0 / jnp.minimum(uq[xk, 0, 0, :, 1024:1025].astype(F32), pc[:, 0:128])
+        for i in range(NI):
+            scq[xk, i] = jnp.broadcast_to(inverse[i : i + 1], (16, 128))
+        return c
+
+    def cross_r(zz):
+        for yk in range(4):
+            def put(i, blk):
+                bw[yk, i] = blk
+
+            blocks(ucr[zz, yk, 0], ucr[zz, yk, 1], put)
+        v = jnp.dot(bw[...].reshape(512, 256), vr[zz].reshape(256, 128), preferred_element_type=F32)
+        v = (v * scr[...].reshape(512, 128)).astype(BF)
+        for yk in range(4):
             for i in range(NI):
-                blk = jnp.where(mask0, a[i : i + 1], jnp.where(mask1, b[i : i + 1], 0.0))
-                bt[g, i // 2, i % 2, pl.ds(k * 16, 16), :] = blk.astype(BF)
-        return c
-
-    lax.fori_loop(0, NP, operand, 0)
-
-    for h in range(2):
-        for k in range(1, NZ):
-            zz = (z + k) % NZ
-            wait_bytes(vg.at[h, zz], v_recv.at[h, zz])
-
-        def cross(ii, c):
-            u = 4 * h + ii
-            scale = jnp.concatenate(
-                [
-                    jnp.broadcast_to(rinv[h, k, pl.ds(2 * ii + par, 1), :], (16, 128))
-                    for par in range(2)
-                    for k in range(NP)
-                ],
-                axis=0,
+                rows = v[(yk * NI + i) * 16 : (yk * NI + i + 1) * 16]
+                lanes = slice((i % 2) * 128, (i % 2 + 1) * 128)
+                if yk:
+                    xsr[zz, yk, i // 2, :, lanes] = rows
+                else:
+                    xrr[i // 2, y, zz, :, lanes] = rows
+        for yk in range(1, 4):
+            remote(
+                xsr.at[zz, yk], xrr.at[:, y, zz], xr_send.at[zz], xr_recv.at[zz],
+                (x * 4 + (y + yk) % 4) * NZ + z, q,
+            ).start()
+
+    def cross_q(zz):
+        for b in range(2):
+            for xk in range(2):
+                def put(i, blk):
+                    bw[2 * b + xk, i] = blk
+
+                blocks(ucq[zz, xk, b, 0], ucq[zz, xk, b, 1], put)
+        for b in range(2):
+            v = jnp.dot(
+                bw[2 * b : 2 * b + 2].reshape(256, 256), vq[zz, 2 * b : 2 * b + 2].reshape(256, 128),
+                preferred_element_type=F32,
             )
-            for g in range(NG):
-                block = vg[h, 2 * g : 2 * g + 2].reshape(256, 128)
-                x = jnp.dot(bt[g, ii].reshape(256, 256), block, preferred_element_type=F32) * scale
-                x = x.astype(BF)
-                for par in range(2):
-                    lanes = slice(par * 128, (par + 1) * 128)
-                    rows = slice(g * 16, (g + 1) * 16)
-                    xr[u, p, rows, lanes] = x[par * 128 : par * 128 + 16]
-                    for k in range(1, NP):
-                        xs[u, k, rows, lanes] = x[par * 128 + k * 16 : par * 128 + (k + 1) * 16]
-            for k in range(1, NP):
-                remote(xs.at[u, k], xr.at[u, p], x_send.at[u], x_recv.at[u], plane(k), q).start()
+            v = (v * scq[...].reshape(256, 128)).astype(BF)
+            for xk in range(2):
+                for i in range(NI):
+                    rows = v[(xk * NI + i) * 16 : (xk * NI + i + 1) * 16]
+                    lanes = slice((i % 2) * 128, (i % 2 + 1) * 128)
+                    if xk:
+                        xsq[zz, i // 2, b, :, lanes] = rows
+                    else:
+                        xrq[i // 2, x, zz, b, :, lanes] = rows
+        remote(xsq.at[zz], xrq.at[:, x, zz], xq_send.at[zz], xq_recv.at[zz], partner, q).start()
+
+    def crossings(cross, start, end):
+        def one(j, c):
+            cross((z + NZ + ((j + 1) // 2) * (2 * (j % 2) - 1)) % NZ)
             return c
 
-        lax.fori_loop(0, 4, cross, 0)
-
-    def flip(g, c):
-        for ii in range(4):
-            for par in range(2):
-                bb[g, par, :, ii * 128 : (ii + 1) * 128] = jnp.transpose(
-                    bt[g, ii, par].astype(F32), (1, 0)
-                ).astype(BF)
-        return c
-
-    lax.fori_loop(0, NG, flip, 0)
+        lax.fori_loop(start, end, one, 0)
+
+    step_r(1)
+    lax.fori_loop(0, 4, ready_r, 0)
+    crossings(cross_r, 0, 1)
+    step_q(1)
+    step_r(2)
+    crossings(cross_r, 1, 3)
+    step_q(2)
+    step_r(3)
+    crossings(cross_r, 3, 5)
+    step_q(3)
+    step_r(4)
+    crossings(cross_r, 5, 8)
+    lax.fori_loop(0, 2, ready_q, 0)
+    crossings(cross_q, 0, 7)
+    step_q(4)
+    crossings(cross_q, 7, 8)
 
     TB = 128
-    loads[NI].wait()
-    loads[NI + 1].wait()
-
-    def pairs(u, c):
-        wait_bytes(xs.at[u, 1:NP], x_recv.at[u])
-        x = xr[u].reshape(2 * F, NJ)
+    for load in loads[NI:]:
+        load.wait()
+
+    def pairs(u, got, mt_ref):
         lo = first[pl.ds(u, 1), :]
         hi = last[pl.ds(u, 1), :]
         for b in range(L // TB):
-            cor = jnp.dot(mt_ref[b * TB : (b + 1) * TB, :], x, preferred_element_type=F32)
-            hil = jnp.dot(mt_ref[L + b * TB : L + (b + 1) * TB, :], x, preferred_element_type=F32)
+            cor = jnp.dot(mt_ref[b * TB : (b + 1) * TB, :], got, preferred_element_type=F32)
+            hil = jnp.dot(mt_ref[L + b * TB : L + (b + 1) * TB, :], got, preferred_element_type=F32)
             rs = lax.rsqrt(cor * cor + hil * hil + env_floor)
             lag = (lax.broadcasted_iota(jnp.int32, (TB, NJ), 0) + b * TB).astype(F32)
             inside = jnp.logical_and(lag >= lo, lag < hi)
@@ -247,12 +350,44 @@
                 zs.at[u, (p + k) % NP], zr.at[:, u, NP - k], z_send.at[u], z_recv.at[u], plane(k), q
             ).start()
         zr[:, u, 0] = zs[u, p]
+
+    def pairs_r(ii, c):
+        pairs(4 + ii, xrr[ii].reshape(2 * F, NJ), mr_ref)
         return c
 
-    lax.fori_loop(0, 8, pairs, 0)
-
-    right = p * NZ + (z + 1) % NZ
-    left = p * NZ + (z + NZ - 1) % NZ
+    def pairs_q(ii, c):
+        pairs(ii, xrq[ii].reshape(2 * F, NJ), mq_ref)
+        return c
+
+    for zz in range(NZ):
+        wait_bytes(xsr.at[zz, 1:4], xr_recv.at[zz])
+    lax.fori_loop(0, 4, pairs_r, 0)
+    for zz in range(NZ):
+        wait_bytes(xsq.at[zz], xq_recv.at[zz])
+    lax.fori_loop(0, 4, pairs_q, 0)
+
+    def operand(k, c):
+        wait_bytes(us.at[k], u_recv.at[k])
+        uf = us[k, :, 0:1024].astype(F32)
+        ut = turned(uf)
+        for g in range(NG):
+            def put(i, blk):
+                bt[g, i // 2, i % 2, pl.ds(k * 16, 16), :] = blk
+
+            blocks(uf[:, g * 256 : (g + 1) * 256], ut[:, g * 256 : (g + 1) * 256], put)
+        return c
+
+    lax.fori_loop(0, NP, operand, 0)
+
+    def flip(g, c):
+        for ii in range(4):
+            for par in range(2):
+                bb[g, par, :, ii * 128 : (ii + 1) * 128] = jnp.transpose(
+                    bt[g, ii, par].astype(F32), (1, 0)
+                ).astype(BF)
+        return c
+
+    lax.fori_loop(0, NG, flip, 0)
 
     def arrived(u):
         wait_bytes(zs.at[u, 1:NP], z_recv.at[u])
@@ -299,7 +434,8 @@
                 t = None
                 for h in range(2):
                     got = zr[g, 4 * h + ii, :, :, par * 128 : (par + 1) * 128].reshape(128, 128)
-                    block = vg[h, 2 * g : 2 * g + 2].reshape(256, 128)
+                    held = vr[2 * g : 2 * g + 2, x] if h else vq[2 * g : 2 * g + 2, y]
+                    block = held.reshape(256, 128)
                     part = lax.dot_general(got, block, nt, preferred_element_type=F32)
                     t = part if t is None else t + part
                 t = t.reshape(NP, 16, 256)
@@ -310,17 +446,17 @@
                 for k in range(NP):
                     rgp[k, i : i + 1, g * 256 : (g + 1) * 256] = rg[k : k + 1]
 
-    for u in range(4):
+    for u in range(4, 8):
         arrived(u)
+    sums(1)
+    ring(1, 0)
+    for s in range(1, 4):
+        arrived(s - 1)
+        receivers(s - 1)
+        ring(1, s)
+    arrived(3)
     sums(0)
     ring(0, 0)
-    for s in range(1, 4):
-        arrived(3 + s)
-        receivers(s - 1)
-        ring(0, s)
-    arrived(7)
-    sums(1)
-    ring(1, 0)
     receivers(3)
     for k in range(NP):
         own = jnp.logical_and(k == 0, p // 2 == q)
@@ -333,16 +469,16 @@
         def _():
             pltpu.make_async_copy(rgp.at[k], rgr.at[q, p % 2], g_recv.at[q, p % 2]).start()
 
-    ring(1, 1)
-    ring_end(0)
-    ring(1, 2)
-    ring(1, 3)
+    ring(0, 1)
+    ring_end(1)
+    ring(0, 2)
+    ring(0, 3)
     for half in range(2):
         for qq in range(4):
             wait_bytes(rgr.at[qq, half], g_recv.at[qq, half])
         total = (rgr[0, half] + rgr[1, half]) + (rgr[2, half] + rgr[3, half])
         rg_out[:, half * 1024 : (half + 1) * 1024] = jnp.where(keep, total, 0.0)
-    ring_end(1)
+    ring_end(0)
 
     for half in range(2):
         for qq in range(4):
@@ -352,10 +488,29 @@
             def _():
                 wait_bytes(um.at[half], u_send.at[half, qq])
 
-    for h in range(2):
-        wait_bytes(vg.at[h, 1:NZ], v_send.at[h])
+    for half in range(2):
+        for qq in range(4):
+            own = jnp.logical_and(2 * (q % 2) + half == y, qq == q)
+
+            @pl.when(jnp.logical_not(own))
+            def _():
+                wait_bytes(um.at[half], ur_send.at[half, qq])
+
+    for qq in range(4):
+        own = jnp.logical_and(q // 2 == x, qq == q)
+
+        @pl.when(jnp.logical_not(own))
+        def _():
+            wait_bytes(um, uq_send.at[qq])
+
+    wait_bytes(vr.at[z, x], vx_send.at[0])
+    wait_bytes(vq.at[z, 1:4], vy_send.at[0])
+    wait_bytes(vr.at[1:NZ], vr_send.at[0])
+    wait_bytes(vq.at[1:NZ], vq_send.at[0])
+    for zz in range(NZ):
+        wait_bytes(xsr.at[zz, 1:4], xr_send.at[zz])
+        wait_bytes(xsq.at[zz], xq_send.at[zz])
     for u in range(8):
-        wait_bytes(xs.at[u, 1:NP], x_send.at[u])
         wait_bytes(zs.at[u, 1:NP], z_send.at[u])
     for k in range(NP):
         own = jnp.logical_and(k == 0, p // 2 == q)
@@ -376,7 +531,11 @@
 def shards(receiver_spectra, reference_spectra, receiver_counts, reference_counts, column_station, lag_window, observed):
     table = lag_table()
     m = jnp.asarray(table, dtype=BF)
-    mt = jnp.asarray(np.ascontiguousarray(table.T), dtype=BF)
+    places = np.arange(2 * F).reshape(2, 4, NZ, 4, 2)
+    order_q = places.transpose(0, 2, 1, 3, 4).reshape(-1)
+    order_r = places.transpose(1, 2, 0, 3, 4).reshape(-1)
+    mq = jnp.asarray(np.ascontiguousarray(table[order_q].T), dtype=BF)
+    mr = jnp.asarray(np.ascontiguousarray(table[order_r].T), dtype=BF)
     vmem = pl.BlockSpec(memory_space=pltpu.VMEM)
     hbm = pl.BlockSpec(memory_space=pl.ANY)
     dma = pltpu.SemaphoreType.DMA
@@ -386,24 +545,34 @@
             pltpu.VMEM((NI, 2048), F32),
             pltpu.VMEM((128, NJ), F32),
         ),
-        in_specs=[vmem] * 6 + [hbm] * 3,
+        in_specs=[vmem] * 6 + [hbm] * 4,
         out_specs=(pl.BlockSpec(memory_space=pltpu.MemorySpace.VMEM), pl.BlockSpec(memory_space=pltpu.MemorySpace.VMEM)),
         scratch_shapes=[
             pltpu.VMEM((2, NI, 1152), BF),
             pltpu.VMEM((NP, NI, 1152), BF),
-            pltpu.VMEM((2, NZ, 128, 128), BF),
+            pltpu.VMEM((4, 2, NI, 1152), BF),
+            pltpu.VMEM((2, 2, 2, NI, 1152), BF),
+            pltpu.VMEM((NZ, 2, 128, 128), BF),
+            pltpu.VMEM((NZ, 4, 128, 128), BF),
+            pltpu.VMEM((NZ, 4, 2, NI, 256), F32),
+            pltpu.VMEM((NZ, 2, 2, 2, NI, 256), F32),
+            pltpu.VMEM((4, NI, 16, 256), BF),
+            pltpu.VMEM((4, NI, 16, 128), F32),
+            pltpu.VMEM((2, NI, 16, 128), F32),
             pltpu.VMEM((NG, 4, 2, 128, 256), BF),
             pltpu.VMEM((NG, 2, 256, 512), BF),
-            pltpu.VMEM((2, NP, NI, 128), F32),
             pltpu.VMEM((8, NJ), F32),
             pltpu.VMEM((8, NJ), F32),
             pltpu.VMEM((8, NJ), F32),
             pltpu.VMEM((NI, NJ, L), BF),
             pltpu.VMEM((2 * F, 2 * L), BF),
             pltpu.VMEM((2 * L, 2 * F), BF),
+            pltpu.VMEM((2 * L, 2 * F), BF),
             pltpu.VMEM((8, L, NJ), BF),
-            pltpu.VMEM((8, NP, 64, NJ), BF),
-            pltpu.VMEM((8, NP, 64, NJ), BF),
+            pltpu.VMEM((NZ, 4, 4, 16, NJ), BF),
+            pltpu.VMEM((4, 4, NZ, 16, NJ), BF),
+            pltpu.VMEM((NZ, 4, 2, 16, NJ), BF),
+            pltpu.VMEM((4, 2, NZ, 2, 16, NJ), BF),
             pltpu.VMEM((2 * L, NJ), BF),
             pltpu.VMEM((8, NP, NG, 16, NJ), BF),
             pltpu.VMEM((NG, 8, NP, 16, NJ), BF),
@@ -412,8 +581,9 @@
             pltpu.VMEM((2, 3, 128, 128), F32),
             pltpu.VMEM((NP, NI, 1024), F32),
             pltpu.VMEM((4, 2, NI, 1024), F32),
-            dma((NI + 2,)), dma((2, 4)), dma((NP,)), dma((2,)), dma((2, NZ)),
-            dma((8,)), dma((8,)), dma((8,)), dma((8,)),
+            dma((NI + 3,)), dma((2, 4)), dma((NP,)), dma((2, 4)), dma((4, 2)), dma((4,)), dma((2, 2)),
+            dma((1,)), dma((1,)), dma((1,)), dma((4,)), dma((1,)), dma((NZ, 2)), dma((1,)), dma((NZ, 4)),
+            dma((NZ,)), dma((NZ,)), dma((NZ,)), dma((NZ,)), dma((8,)), dma((8,)),
             dma((NP,)), dma((4, 2)), dma((2, 4, 2)), dma((2, 4, 2)), dma((2, 3, 2)), dma((2, 3, 2)),
         ],
         compiler_params=pltpu.CompilerParams(
@@ -428,7 +598,8 @@
         lag_window,
         observed,
         m,
-        mt,
+        mq,
+        mr,
     )
 
 

time: 87.5 us -> 84.9 us (0.970)
  Pallas kernels: 84.8 us -> 82.5 us
    pallas_call x1, Pallas kernels: 84.8 us -> 82.5 us  [shards(): pl.pallas_call(kernel, out_shape=(pltpu.VMEM((NI, 2048), F32), pltpu.VMEM...]
where the time goes in v4:
time: 84.9 us; the launch traced here: 84.5 us
  Pallas kernels  82.5 us (97%)
  local copies, waits for them, and re-layouts  1.29 us (2%)
    pallas_call x1, Pallas kernels, shards(): pl.pallas_call(kernel, out_shape=(pltpu.VMEM((NI, 2048), F32), pltpu.VMEM...  82.5 us

profile of v4, /device:TPU:2, one launch (start us, length us, event | category | flops | bytes accessed | tf_op | source)
XLA Modules:
  0.0 84.5 jit_solution(4939917881995199263)
XLA Ops:
  0.6 82.5 %shard_map.113 = (f32[8,2048]{1,0:T(8,128)S(1)}, f32[128,256]{1,0:T(8,128)S(1)}) custom-call(bf16[8,2048]{1,0:T(8,128)(2,1)} %u_ref.1, bf16[128,256]{1,0:T(8,128)(2,1)} %v_ref.1, s32[1,8]{1,0:T(1,128)} %bitcast.5, s32[1,256]{1,0:T(1,128)} %bitcast.3, s32[1,256]{1,0:T(1,128)} %bitcast.4, s32[2,8,256]{2,1,0:T(8,128)} %win_ref.1, bf16[8,256,512]{2,1,0:T(8,128)(2,1)} %obs_hbm.1, ...), custom_call_target="tpu_custom_call" | custom-call | tf_op jit(solution)/shard_map/pallas_call | solution.py:542
  83.2 0.6 copy.14
  83.8 0.7 copy.15

commit v5 on v4

--- a/solution.py
+++ b/solution.py
@@ -15,6 +15,7 @@
 NZ = 8
 NI = 8
 NJ = 256
+NS = 4
 NG = 4
 MESH = pl.DeviceIdType.MESH
 BF = jnp.bfloat16
@@ -37,10 +38,10 @@
 
 
 def kernel(
-    u_ref, v_ref, rc_ref, fc_ref, cs_ref, win_ref, obs_hbm, m_hbm, mq_hbm, mr_hbm,
+    u_ref, v_ref, rc_ref, fc_ref, cs_ref, win_ref, obs_hbm, m_hbm, mt_hbm,
     rg_out, wg_out,
     um, us, ur, uq, vr, vq, ucr, ucq, bw, scr, scq, bt, bb, ninv, first, last,
-    obs, m_ref, mq_ref, mr_ref, obst, xsr, xrr, xsq, xrq, gs, zs, zr,
+    obs, m_ref, mt_ref, mq_ref, mr_ref, obst, xsr, xrr, xsq, xrq, gs, zs, zr,
     w, rbuf, lbuf, rgp, rgr,
     in_sem, u_send, u_recv, ur_send, ur_recv, uq_send, uq_recv,
     vx_send, vx_recv, vy_send, vy_recv, vr_send, vr_recv, vq_send, vq_recv,
@@ -81,9 +82,8 @@
     signal(left, q)
 
     loads = [pltpu.make_async_copy(obs_hbm.at[i], obs.at[i], in_sem.at[i]) for i in range(NI)]
-    loads.append(pltpu.make_async_copy(mr_hbm, mr_ref, in_sem.at[NI]))
+    loads.append(pltpu.make_async_copy(mt_hbm, mt_ref, in_sem.at[NI]))
     loads.append(pltpu.make_async_copy(m_hbm, m_ref, in_sem.at[NI + 1]))
-    loads.append(pltpu.make_async_copy(mq_hbm, mq_ref, in_sem.at[NI + 2]))
     for load in loads:
         load.start()
 
@@ -100,32 +100,6 @@
         part = u_ref[:, half * 1024 : (half + 1) * 1024].astype(F32)
         um[half, :, 0:1024] = jnp.where(keep, part, 0.0).astype(BF)
         um[half, :, 1024:1152] = jnp.broadcast_to(rcounts, (NI, 128)).astype(BF)
-
-    order = cs_ref[...] - q * NJ
-    stations = lax.broadcasted_iota(jnp.int32, (NJ, NJ), 0)
-    onehot = jnp.where(stations == order, 1.0, 0.0).astype(BF)
-    nt = (((1,), (1,)), ((), ()))
-    begin = lax.dot_general(win_ref[0].astype(F32).astype(BF), onehot, nt, preferred_element_type=F32)
-    span = lax.dot_general(win_ref[1].astype(F32).astype(BF), onehot, nt, preferred_element_type=F32)
-    inv = 1.0 / jnp.minimum(rcounts, pc)
-    for h in range(2):
-        for i in range(NI):
-            u, lanes, side = 4 * h + i // 2, pl.ds((i % 2) * 128, 128), slice(h * 128, (h + 1) * 128)
-            first[u : u + 1, lanes] = begin[i : i + 1, side]
-            last[u : u + 1, lanes] = begin[i : i + 1, side] + span[i : i + 1, side]
-            ninv[u : u + 1, lanes] = inv[i : i + 1, side]
-    for i in range(NI):
-        loads[i].wait()
-
-    def turn(ii, c):
-        for par in range(2):
-            seen = jnp.dot(onehot, obs[2 * ii + par], preferred_element_type=F32)
-            seen = jnp.transpose(seen, (1, 0)).astype(BF)
-            for h in range(2):
-                obst[4 * h + ii, :, par * 128 : (par + 1) * 128] = seen[:, h * 128 : (h + 1) * 128]
-        return c
-
-    lax.fori_loop(0, NI // 2, turn, 0)
 
     pl.semaphore_wait(barrier, 4 * NP - 1 + 2)
 
@@ -171,6 +145,31 @@
             own, um, uq.at[(x - xd + 2) % 2, q % 2], uq_send.at[qq],
             uq_recv.at[(x - xd + 2) % 2, q % 2], (xd * 4 + y) * NZ + z, qq,
         )
+    order = cs_ref[...] - q * NJ
+    stations = lax.broadcasted_iota(jnp.int32, (NJ, NJ), 0)
+    onehot = jnp.where(stations == order, 1.0, 0.0).astype(BF)
+    nt = (((1,), (1,)), ((), ()))
+    begin = lax.dot_general(win_ref[0].astype(F32).astype(BF), onehot, nt, preferred_element_type=F32)
+    span = lax.dot_general(win_ref[1].astype(F32).astype(BF), onehot, nt, preferred_element_type=F32)
+    inv = 1.0 / jnp.minimum(rcounts, pc)
+    for h in range(2):
+        for i in range(NI):
+            u, lanes, side = 4 * h + i // 2, pl.ds((i % 2) * 128, 128), slice(h * 128, (h + 1) * 128)
+            first[u : u + 1, lanes] = begin[i : i + 1, side]
+            last[u : u + 1, lanes] = begin[i : i + 1, side] + span[i : i + 1, side]
+            ninv[u : u + 1, lanes] = inv[i : i + 1, side]
+    def turn(ii, c):
+        for par in range(2):
+            seen = jnp.dot(onehot, obs[2 * ii + par], preferred_element_type=F32)
+            seen = jnp.transpose(seen, (1, 0)).astype(BF)
+            for h in range(2):
+                obst[4 * h + ii, :, par * 128 : (par + 1) * 128] = seen[:, h * 128 : (h + 1) * 128]
+        return c
+
+    for i in range(NI):
+        loads[i].wait()
+    lax.fori_loop(0, 2, turn, 0)
+
     wait_bytes(vr.at[z, 1 - x], vx_recv.at[0])
     pass_r(z, 1 - x, right)
     pass_r(z, 1 - x, left)
@@ -307,33 +306,46 @@
 
         lax.fori_loop(start, end, one, 0)
 
+    lax.fori_loop(2, 4, turn, 0)
     step_r(1)
     lax.fori_loop(0, 4, ready_r, 0)
-    crossings(cross_r, 0, 1)
+    crossings(cross_r, 0, 3)
     step_q(1)
+    lax.fori_loop(0, 2, ready_q, 0)
+    crossings(cross_q, 0, 3)
     step_r(2)
-    crossings(cross_r, 1, 3)
+    crossings(cross_r, 3, 5)
     step_q(2)
+    crossings(cross_q, 3, 5)
     step_r(3)
-    crossings(cross_r, 3, 5)
+    crossings(cross_r, 5, 7)
     step_q(3)
+    crossings(cross_q, 5, 7)
     step_r(4)
-    crossings(cross_r, 5, 8)
-    lax.fori_loop(0, 2, ready_q, 0)
-    crossings(cross_q, 0, 7)
+    crossings(cross_r, 7, 8)
+
+    for load in loads[NI:]:
+        load.wait()
+    here = lax.broadcasted_iota(jnp.int32, (2 * F, 2 * F), 0)
+    n = lax.broadcasted_iota(jnp.int32, (2 * F, 2 * F), 1)
+    from_r = n % 8 + 8 * ((n // 16) % 8) + 64 * (n // 128) + 256 * ((n // 8) % 2)
+    from_q = n % 8 + 8 * ((n // 32) % 8) + 64 * ((n // 8) % 4) + 256 * (n // 256)
+    for source, out in ((from_r, mr_ref), (from_q, mq_ref)):
+        pick = jnp.where(here == source, 1.0, 0.0).astype(BF)
+        for b in range(4):
+            rows = slice(b * 256, (b + 1) * 256)
+            out[rows, :] = jnp.dot(mt_ref[rows, :], pick, preferred_element_type=F32).astype(BF)
+
     step_q(4)
     crossings(cross_q, 7, 8)
 
     TB = 128
-    for load in loads[NI:]:
-        load.wait()
-
-    def pairs(u, got, mt_ref):
+    def pairs(u, got, table):
         lo = first[pl.ds(u, 1), :]
         hi = last[pl.ds(u, 1), :]
         for b in range(L // TB):
-            cor = jnp.dot(mt_ref[b * TB : (b + 1) * TB, :], got, preferred_element_type=F32)
-            hil = jnp.dot(mt_ref[L + b * TB : L + (b + 1) * TB, :], got, preferred_element_type=F32)
+            cor = jnp.dot(table[b * TB : (b + 1) * TB, :], got, preferred_element_type=F32)
+            hil = jnp.dot(table[L + b * TB : L + (b + 1) * TB, :], got, preferred_element_type=F32)
             rs = lax.rsqrt(cor * cor + hil * hil + env_floor)
             lag = (lax.broadcasted_iota(jnp.int32, (TB, NJ), 0) + b * TB).astype(F32)
             inside = jnp.logical_and(lag >= lo, lag < hi)
@@ -392,18 +404,22 @@
     def arrived(u):
         wait_bytes(zs.at[u, 1:NP], z_recv.at[u])
 
-    def sums(h):
+    def sums(h, start, end):
+        size = (end - start) * 128
         for g in range(NG):
-            part = jnp.dot(
-                bb[g, 0], zr[g, 4 * h : 4 * h + 4, :, :, 0:128].reshape(512, 128), preferred_element_type=F32
-            ) + jnp.dot(
-                bb[g, 1], zr[g, 4 * h : 4 * h + 4, :, :, 128:256].reshape(512, 128), preferred_element_type=F32
-            )
-            w[h, 2 * g : 2 * g + 2] = part.reshape(2, 128, 128)
+            part = None
+            for par in range(2):
+                got = zr[g, 4 * h + start : 4 * h + end, :, :, par * 128 : (par + 1) * 128].reshape(size, 128)
+                one = jnp.dot(bb[g, par, :, start * 128 : end * 128], got, preferred_element_type=F32)
+                part = one if part is None else part + one
+            part = part.reshape(2, 128, 128)
+            if start:
+                part = part + w[h, 2 * g : 2 * g + 2]
+            w[h, 2 * g : 2 * g + 2] = part
 
     def ring(h, s):
-        for n in range(2):
-            rows = slice(n * 64, (n + 1) * 64)
+        for n in range(NS):
+            rows = slice(n * (128 // NS), (n + 1) * (128 // NS))
             if s > 0:
                 wait_bytes(rbuf.at[h, s - 1, rows], r_recv.at[h, s - 1, n])
                 rbuf[h, s - 1, rows] = rbuf[h, s - 1, rows] + w[h, (z + 4 - s) % NZ, rows]
@@ -418,8 +434,8 @@
             remote(src, lbuf.at[h, s, rows], l_send.at[h, s, n], l_recv.at[h, s, n], left, q).start()
 
     def ring_end(h):
-        for n in range(2):
-            rows = slice(n * 64, (n + 1) * 64)
+        for n in range(NS):
+            rows = slice(n * (128 // NS), (n + 1) * (128 // NS))
             wait_bytes(rbuf.at[h, 3, rows], r_recv.at[h, 3, n])
             wait_bytes(lbuf.at[h, 2, rows], l_recv.at[h, 2, n])
             keep = row_mask[rows, h * 128 : (h + 1) * 128]
@@ -448,14 +464,15 @@
 
     for u in range(4, 8):
         arrived(u)
-    sums(1)
+    sums(1, 0, 4)
     ring(1, 0)
     for s in range(1, 4):
         arrived(s - 1)
         receivers(s - 1)
         ring(1, s)
+    sums(0, 0, 3)
     arrived(3)
-    sums(0)
+    sums(0, 3, 4)
     ring(0, 0)
     receivers(3)
     for k in range(NP):
@@ -520,8 +537,8 @@
             wait_bytes(rgp.at[k], g_send.at[k])
 
     for h in range(2):
-        for n in range(2):
-            rows = slice(n * 64, (n + 1) * 64)
+        for n in range(NS):
+            rows = slice(n * (128 // NS), (n + 1) * (128 // NS))
             for s in range(4):
                 wait_bytes(rbuf.at[h, s, rows], r_send.at[h, s, n])
             for s in range(3):
@@ -531,11 +548,7 @@
 def shards(receiver_spectra, reference_spectra, receiver_counts, reference_counts, column_station, lag_window, observed):
     table = lag_table()
     m = jnp.asarray(table, dtype=BF)
-    places = np.arange(2 * F).reshape(2, 4, NZ, 4, 2)
-    order_q = places.transpose(0, 2, 1, 3, 4).reshape(-1)
-    order_r = places.transpose(1, 2, 0, 3, 4).reshape(-1)
-    mq = jnp.asarray(np.ascontiguousarray(table[order_q].T), dtype=BF)
-    mr = jnp.asarray(np.ascontiguousarray(table[order_r].T), dtype=BF)
+    mt = jnp.asarray(np.ascontiguousarray(table.T), dtype=BF)
     vmem = pl.BlockSpec(memory_space=pltpu.VMEM)
     hbm = pl.BlockSpec(memory_space=pl.ANY)
     dma = pltpu.SemaphoreType.DMA
@@ -545,7 +558,7 @@
             pltpu.VMEM((NI, 2048), F32),
             pltpu.VMEM((128, NJ), F32),
         ),
-        in_specs=[vmem] * 6 + [hbm] * 4,
+        in_specs=[vmem] * 6 + [hbm] * 3,
         out_specs=(pl.BlockSpec(memory_space=pltpu.MemorySpace.VMEM), pl.BlockSpec(memory_space=pltpu.MemorySpace.VMEM)),
         scratch_shapes=[
             pltpu.VMEM((2, NI, 1152), BF),
@@ -568,6 +581,7 @@
             pltpu.VMEM((2 * F, 2 * L), BF),
             pltpu.VMEM((2 * L, 2 * F), BF),
             pltpu.VMEM((2 * L, 2 * F), BF),
+            pltpu.VMEM((2 * L, 2 * F), BF),
             pltpu.VMEM((8, L, NJ), BF),
             pltpu.VMEM((NZ, 4, 4, 16, NJ), BF),
             pltpu.VMEM((4, 4, NZ, 16, NJ), BF),
@@ -581,10 +595,10 @@
             pltpu.VMEM((2, 3, 128, 128), F32),
             pltpu.VMEM((NP, NI, 1024), F32),
             pltpu.VMEM((4, 2, NI, 1024), F32),
-            dma((NI + 3,)), dma((2, 4)), dma((NP,)), dma((2, 4)), dma((4, 2)), dma((4,)), dma((2, 2)),
+            dma((NI + 2,)), dma((2, 4)), dma((NP,)), dma((2, 4)), dma((4, 2)), dma((4,)), dma((2, 2)),
             dma((1,)), dma((1,)), dma((1,)), dma((4,)), dma((1,)), dma((NZ, 2)), dma((1,)), dma((NZ, 4)),
             dma((NZ,)), dma((NZ,)), dma((NZ,)), dma((NZ,)), dma((8,)), dma((8,)),
-            dma((NP,)), dma((4, 2)), dma((2, 4, 2)), dma((2, 4, 2)), dma((2, 3, 2)), dma((2, 3, 2)),
+            dma((NP,)), dma((4, 2)), dma((2, 4, NS)), dma((2, 4, NS)), dma((2, 3, NS)), dma((2, 3, NS)),
         ],
         compiler_params=pltpu.CompilerParams(
             collective_id=0, has_side_effects=True, vmem_limit_bytes=60 * 1024 * 1024
@@ -598,8 +612,7 @@
         lag_window,
         observed,
         m,
-        mq,
-        mr,
+        mt,
     )
 
 

time: 84.9 us -> 79.2 us (0.933)
  Pallas kernels: 82.5 us -> 77.1 us
    pallas_call x1, Pallas kernels: 82.5 us -> 77.1 us  [shards(): pl.pallas_call(kernel, out_shape=(pltpu.VMEM((NI, 2048), F32), pltpu.VMEM...]
where the time goes in v5:
time: 79.2 us; the launch traced here: 79.1 us
  Pallas kernels  77.1 us (97%)
  local copies, waits for them, and re-layouts  1.29 us (2%)
    pallas_call x1, Pallas kernels, shards(): pl.pallas_call(kernel, out_shape=(pltpu.VMEM((NI, 2048), F32), pltpu.VMEM...  77.1 us

profile of v5, /device:TPU:2, one launch (start us, length us, event | category | flops | bytes accessed | tf_op | source)
XLA Modules:
  0.0 79.1 jit_solution(3069363951533661056)
XLA Ops:
  0.6 77.1 %shard_map.104 = (f32[8,2048]{1,0:T(8,128)S(1)}, f32[128,256]{1,0:T(8,128)S(1)}) custom-call(bf16[8,2048]{1,0:T(8,128)(2,1)} %u_ref.1, bf16[128,256]{1,0:T(8,128)(2,1)} %v_ref.1, s32[1,8]{1,0:T(1,128)} %bitcast.5, s32[1,256]{1,0:T(1,128)} %bitcast.3, s32[1,256]{1,0:T(1,128)} %bitcast.4, s32[2,8,256]{2,1,0:T(8,128)} %win_ref.1, bf16[8,256,512]{2,1,0:T(8,128)(2,1)} %obs_hbm.1, ...), custom_call_target="tpu_custom_call" | custom-call | tf_op jit(solution)/shard_map/pallas_call | solution.py:555
  77.8 0.6 copy.13
  78.4 0.7 copy.14

commit v6 on v5

--- a/solution.py
+++ b/solution.py
@@ -15,7 +15,6 @@
 NZ = 8
 NI = 8
 NJ = 256
-NS = 4
 NG = 4
 MESH = pl.DeviceIdType.MESH
 BF = jnp.bfloat16
@@ -42,11 +41,11 @@
     rg_out, wg_out,
     um, us, ur, uq, vr, vq, ucr, ucq, bw, scr, scq, bt, bb, ninv, first, last,
     obs, m_ref, mt_ref, mq_ref, mr_ref, obst, xsr, xrr, xsq, xrq, gs, zs, zr,
-    w, rbuf, lbuf, rgp, rgr,
+    w, tbuf, rgp, rgr,
     in_sem, u_send, u_recv, ur_send, ur_recv, uq_send, uq_recv,
     vx_send, vx_recv, vy_send, vy_recv, vr_send, vr_recv, vq_send, vq_recv,
     xr_send, xr_recv, xq_send, xq_recv, z_send, z_recv,
-    g_send, g_recv, r_send, r_recv, l_send, l_recv,
+    g_send, g_recv, t_send, t_recv,
 ):
     r = lax.axis_index("rcv")
     q = lax.axis_index("ref")
@@ -78,12 +77,12 @@
         for dq in range(4):
             if k or dq:
                 signal(plane(k), (q + dq) % 4)
-    signal(right, q)
-    signal(left, q)
-
-    loads = [pltpu.make_async_copy(obs_hbm.at[i], obs.at[i], in_sem.at[i]) for i in range(NI)]
-    loads.append(pltpu.make_async_copy(mt_hbm, mt_ref, in_sem.at[NI]))
-    loads.append(pltpu.make_async_copy(m_hbm, m_ref, in_sem.at[NI + 1]))
+    for k in (1, 2, 6, 7):
+        signal(p * NZ + (z + k) % NZ, q)
+
+    loads = [pltpu.make_async_copy(obs_hbm.at[i], obs.at[i], in_sem.at[0]) for i in range(NI)]
+    loads.append(pltpu.make_async_copy(mt_hbm, mt_ref, in_sem.at[1]))
+    loads.append(pltpu.make_async_copy(m_hbm, m_ref, in_sem.at[2]))
     for load in loads:
         load.start()
 
@@ -101,7 +100,7 @@
         um[half, :, 0:1024] = jnp.where(keep, part, 0.0).astype(BF)
         um[half, :, 1024:1152] = jnp.broadcast_to(rcounts, (NI, 128)).astype(BF)
 
-    pl.semaphore_wait(barrier, 4 * NP - 1 + 2)
+    pl.semaphore_wait(barrier, 4 * NP - 1 + 4)
 
     def give(own, src, dst, send, recv, rr, qq):
         @pl.when(jnp.logical_not(own))
@@ -135,15 +134,15 @@
             yd = 2 * (q % 2) + half
             own = jnp.logical_and(yd == y, qq == q)
             give(
-                own, um.at[half], ur.at[(y - yd + 4) % 4, q // 2], ur_send.at[half, qq],
-                ur_recv.at[(y - yd + 4) % 4, q // 2], (x * 4 + yd) * NZ + z, qq,
+                own, um.at[half], ur.at[(y - yd + 4) % 4, q // 2], ur_send.at[0], ur_recv.at[0],
+                (x * 4 + yd) * NZ + z, qq,
             )
     for qq in range(4):
         xd = q // 2
         own = jnp.logical_and(xd == x, qq == q)
         give(
-            own, um, uq.at[(x - xd + 2) % 2, q % 2], uq_send.at[qq],
-            uq_recv.at[(x - xd + 2) % 2, q % 2], (xd * 4 + y) * NZ + z, qq,
+            own, um, uq.at[2 * ((x - xd + 2) % 2) + q % 2], uq_send.at[0], uq_recv.at[0],
+            (xd * 4 + y) * NZ + z, qq,
         )
     order = cs_ref[...] - q * NJ
     stations = lax.broadcasted_iota(jnp.int32, (NJ, NJ), 0)
@@ -166,8 +165,7 @@
                 obst[4 * h + ii, :, par * 128 : (par + 1) * 128] = seen[:, h * 128 : (h + 1) * 128]
         return c
 
-    for i in range(NI):
-        loads[i].wait()
+    wait_bytes(obs, in_sem.at[0])
     lax.fori_loop(0, 2, turn, 0)
 
     wait_bytes(vr.at[z, 1 - x], vx_recv.at[0])
@@ -184,7 +182,7 @@
             rr = pp * NZ + z
             own = jnp.logical_and(rr == r, qq == q)
             slot = (p - pp + NP) % NP
-            give(own, um.at[half], us.at[slot], u_send.at[half, qq], u_recv.at[slot], rr, qq)
+            give(own, um.at[half], us.at[slot], u_send.at[0], u_recv.at[0], rr, qq)
 
     def back(s):
         return (z + NZ - s) % NZ
@@ -229,7 +227,6 @@
 
     def ready_r(yk, c):
         for xx in range(2):
-            wait_bytes(ur.at[yk, xx], ur_recv.at[yk, xx])
             uf = ur[yk, xx, :, 0:1024].astype(F32)
             ut = turned(uf)
             for zz in range(NZ):
@@ -242,14 +239,13 @@
 
     def ready_q(xk, c):
         for b in range(2):
-            wait_bytes(uq.at[xk, b], uq_recv.at[xk, b])
             for half in range(2):
-                uf = uq[xk, b, half, :, 0:1024].astype(F32)
+                uf = uq[2 * xk + b, half, :, 0:1024].astype(F32)
                 ut = turned(uf)
                 for zz in range(NZ):
                     ucq[zz, xk, b, 0, :, half * 128 : (half + 1) * 128] = uf[:, zz * 128 : (zz + 1) * 128]
                     ucq[zz, xk, b, 1, :, half * 128 : (half + 1) * 128] = ut[:, zz * 128 : (zz + 1) * 128]
-        inverse = 1.0 / jnp.minimum(uq[xk, 0, 0, :, 1024:1025].astype(F32), pc[:, 0:128])
+        inverse = 1.0 / jnp.minimum(uq[2 * xk, 0, :, 1024:1025].astype(F32), pc[:, 0:128])
         for i in range(NI):
             scq[xk, i] = jnp.broadcast_to(inverse[i : i + 1], (16, 128))
         return c
@@ -272,7 +268,7 @@
                     xrr[i // 2, y, zz, :, lanes] = rows
         for yk in range(1, 4):
             remote(
-                xsr.at[zz, yk], xrr.at[:, y, zz], xr_send.at[zz], xr_recv.at[zz],
+                xsr.at[zz, yk], xrr.at[:, y, zz], xr_send.at[0], xr_recv.at[0],
                 (x * 4 + (y + yk) % 4) * NZ + z, q,
             ).start()
 
@@ -297,7 +293,7 @@
                         xsq[zz, i // 2, b, :, lanes] = rows
                     else:
                         xrq[i // 2, x, zz, b, :, lanes] = rows
-        remote(xsq.at[zz], xrq.at[:, x, zz], xq_send.at[zz], xq_recv.at[zz], partner, q).start()
+        remote(xsq.at[zz], xrq.at[:, x, zz], xq_send.at[0], xq_recv.at[0], partner, q).start()
 
     def crossings(cross, start, end):
         def one(j, c):
@@ -308,36 +304,39 @@
 
     lax.fori_loop(2, 4, turn, 0)
     step_r(1)
+    wait_bytes(ur, ur_recv.at[0])
     lax.fori_loop(0, 4, ready_r, 0)
     crossings(cross_r, 0, 3)
+    step_r(2)
+    crossings(cross_r, 3, 5)
     step_q(1)
+    wait_bytes(uq, uq_recv.at[0])
     lax.fori_loop(0, 2, ready_q, 0)
     crossings(cross_q, 0, 3)
-    step_r(2)
-    crossings(cross_r, 3, 5)
+    step_r(3)
+    crossings(cross_r, 5, 7)
     step_q(2)
     crossings(cross_q, 3, 5)
-    step_r(3)
-    crossings(cross_r, 5, 7)
-    step_q(3)
-    crossings(cross_q, 5, 7)
-    step_r(4)
-    crossings(cross_r, 7, 8)
-
-    for load in loads[NI:]:
-        load.wait()
+
     here = lax.broadcasted_iota(jnp.int32, (2 * F, 2 * F), 0)
     n = lax.broadcasted_iota(jnp.int32, (2 * F, 2 * F), 1)
     from_r = n % 8 + 8 * ((n // 16) % 8) + 64 * (n // 128) + 256 * ((n // 8) % 2)
     from_q = n % 8 + 8 * ((n // 32) % 8) + 64 * ((n // 8) % 4) + 256 * (n // 256)
-    for source, out in ((from_r, mr_ref), (from_q, mq_ref)):
+
+    def reorder(source, out):
         pick = jnp.where(here == source, 1.0, 0.0).astype(BF)
         for b in range(4):
             rows = slice(b * 256, (b + 1) * 256)
             out[rows, :] = jnp.dot(mt_ref[rows, :], pick, preferred_element_type=F32).astype(BF)
 
-    step_q(4)
-    crossings(cross_q, 7, 8)
+    for load in loads[NI:]:
+        load.wait()
+    reorder(from_r, mr_ref)
+    step_r(4)
+    crossings(cross_r, 7, 8)
+    step_q(3)
+    crossings(cross_q, 5, 7)
+    reorder(from_q, mq_ref)
 
     TB = 128
     def pairs(u, got, table):
@@ -357,9 +356,9 @@
         for b in range(4):
             back = jnp.dot(m_ref[b * 128 : (b + 1) * 128, :], gs[...], preferred_element_type=F32)
             zs[u, 2 * b : 2 * b + 2] = (back * scale).astype(BF).reshape(2, NG, 16, NJ)
-        for k in range(1, NP):
+        for k in (4, 5, 7, 6, 1, 3, 2):
             remote(
-                zs.at[u, (p + k) % NP], zr.at[:, u, NP - k], z_send.at[u], z_recv.at[u], plane(k), q
+                zs.at[u, (p + k) % NP], zr.at[:, u, NP - k], z_send.at[u // 4], z_recv.at[u], plane(k), q
             ).start()
         zr[:, u, 0] = zs[u, p]
 
@@ -371,15 +370,14 @@
         pairs(ii, xrq[ii].reshape(2 * F, NJ), mq_ref)
         return c
 
-    for zz in range(NZ):
-        wait_bytes(xsr.at[zz, 1:4], xr_recv.at[zz])
+    wait_bytes(xsr.at[:, 1:4], xr_recv.at[0])
     lax.fori_loop(0, 4, pairs_r, 0)
-    for zz in range(NZ):
-        wait_bytes(xsq.at[zz], xq_recv.at[zz])
+    step_q(4)
+    crossings(cross_q, 7, 8)
+    wait_bytes(xsq, xq_recv.at[0])
     lax.fori_loop(0, 4, pairs_q, 0)
 
     def operand(k, c):
-        wait_bytes(us.at[k], u_recv.at[k])
         uf = us[k, :, 0:1024].astype(F32)
         ut = turned(uf)
         for g in range(NG):
@@ -389,6 +387,7 @@
             blocks(uf[:, g * 256 : (g + 1) * 256], ut[:, g * 256 : (g + 1) * 256], put)
         return c
 
+    wait_bytes(us, u_recv.at[0])
     lax.fori_loop(0, NP, operand, 0)
 
     def flip(g, c):
@@ -417,30 +416,28 @@
                 part = part + w[h, 2 * g : 2 * g + 2]
             w[h, 2 * g : 2 * g + 2] = part
 
-    def ring(h, s):
-        for n in range(NS):
-            rows = slice(n * (128 // NS), (n + 1) * (128 // NS))
-            if s > 0:
-                wait_bytes(rbuf.at[h, s - 1, rows], r_recv.at[h, s - 1, n])
-                rbuf[h, s - 1, rows] = rbuf[h, s - 1, rows] + w[h, (z + 4 - s) % NZ, rows]
-            src = rbuf.at[h, s - 1, rows] if s > 0 else w.at[h, (z + 4) % NZ, rows]
-            remote(src, rbuf.at[h, s, rows], r_send.at[h, s, n], r_recv.at[h, s, n], right, q).start()
-            if s > 2:
-                continue
-            if s > 0:
-                wait_bytes(lbuf.at[h, s - 1, rows], l_recv.at[h, s - 1, n])
-                lbuf[h, s - 1, rows] = lbuf[h, s - 1, rows] + w[h, (z + 5 + s) % NZ, rows]
-            src = lbuf.at[h, s - 1, rows] if s > 0 else w.at[h, (z + 5) % NZ, rows]
-            remote(src, lbuf.at[h, s, rows], l_send.at[h, s, n], l_recv.at[h, s, n], left, q).start()
-
-    def ring_end(h):
-        for n in range(NS):
-            rows = slice(n * (128 // NS), (n + 1) * (128 // NS))
-            wait_bytes(rbuf.at[h, 3, rows], r_recv.at[h, 3, n])
-            wait_bytes(lbuf.at[h, 2, rows], l_recv.at[h, 2, n])
-            keep = row_mask[rows, h * 128 : (h + 1) * 128]
-            done = w[h, z, rows] + rbuf[h, 3, rows] + lbuf[h, 2, rows]
-            wg_out[rows, h * 128 : (h + 1) * 128] = jnp.where(keep, done, 0.0)
+    def toward(n, src, dst, h, to):
+        remote(src, dst, t_send.at[h], t_recv.at[h, n], p * NZ + (z + NZ + to) % NZ, q).start()
+
+    def tree_start(h):
+        for n, m, to in ((0, 4, 2), (1, 3, 1), (2, 5, -1), (3, 1, 1), (4, 7, -1)):
+            toward(n, w.at[h, (z + m) % NZ], tbuf.at[h, n], h, to)
+
+    def tree_middle(h):
+        wait_bytes(tbuf.at[h, 2], t_recv.at[h, 2])
+        tbuf[h, 2] = tbuf[h, 2] + w[h, (z + 6) % NZ]
+        toward(6, tbuf.at[h, 2], tbuf.at[h, 6], h, -2)
+        wait_bytes(tbuf.at[h, 1], t_recv.at[h, 1])
+        wait_bytes(tbuf.at[h, 0], t_recv.at[h, 0])
+        tbuf[h, 0] = tbuf[h, 0] + (tbuf[h, 1] + w[h, (z + 2) % NZ])
+        toward(5, tbuf.at[h, 0], tbuf.at[h, 5], h, 2)
+
+    def tree_end(h):
+        for n in (3, 4, 6, 5):
+            wait_bytes(tbuf.at[h, n], t_recv.at[h, n])
+        done = (w[h, z] + tbuf[h, 3]) + (tbuf[h, 4] + tbuf[h, 6]) + tbuf[h, 5]
+        cols = slice(h * 128, (h + 1) * 128)
+        wg_out[:, cols] = jnp.where(row_mask[:, cols], done, 0.0)
 
     lane8 = (lax.broadcasted_iota(jnp.int32, (NP, 256), 1) // S) % 2
 
@@ -465,84 +462,62 @@
     for u in range(4, 8):
         arrived(u)
     sums(1, 0, 4)
-    ring(1, 0)
-    for s in range(1, 4):
-        arrived(s - 1)
-        receivers(s - 1)
-        ring(1, s)
+    tree_start(1)
+    arrived(0)
+    receivers(0)
+    tree_middle(1)
+    arrived(1)
+    receivers(1)
+    arrived(2)
+    receivers(2)
     sums(0, 0, 3)
+    tree_end(1)
     arrived(3)
     sums(0, 3, 4)
-    ring(0, 0)
+    tree_start(0)
     receivers(3)
     for k in range(NP):
         own = jnp.logical_and(k == 0, p // 2 == q)
 
         @pl.when(jnp.logical_not(own))
         def _():
-            remote(rgp.at[k], rgr.at[q, p % 2], g_send.at[k], g_recv.at[q, p % 2], plane(k), p // 2).start()
+            remote(rgp.at[k], rgr.at[q, p % 2], g_send.at[0], g_recv.at[0], plane(k), p // 2).start()
 
         @pl.when(own)
         def _():
-            pltpu.make_async_copy(rgp.at[k], rgr.at[q, p % 2], g_recv.at[q, p % 2]).start()
-
-    ring(0, 1)
-    ring_end(1)
-    ring(0, 2)
-    ring(0, 3)
+            pltpu.make_async_copy(rgp.at[k], rgr.at[q, p % 2], g_recv.at[0]).start()
+
+    tree_middle(0)
+    wait_bytes(rgr, g_recv.at[0])
     for half in range(2):
-        for qq in range(4):
-            wait_bytes(rgr.at[qq, half], g_recv.at[qq, half])
         total = (rgr[0, half] + rgr[1, half]) + (rgr[2, half] + rgr[3, half])
         rg_out[:, half * 1024 : (half + 1) * 1024] = jnp.where(keep, total, 0.0)
-    ring_end(0)
-
-    for half in range(2):
-        for qq in range(4):
-            own = jnp.logical_and((2 * q + half) * NZ + z == r, qq == q)
-
-            @pl.when(jnp.logical_not(own))
-            def _():
-                wait_bytes(um.at[half], u_send.at[half, qq])
-
-    for half in range(2):
-        for qq in range(4):
-            own = jnp.logical_and(2 * (q % 2) + half == y, qq == q)
-
-            @pl.when(jnp.logical_not(own))
-            def _():
-                wait_bytes(um.at[half], ur_send.at[half, qq])
-
-    for qq in range(4):
-        own = jnp.logical_and(q // 2 == x, qq == q)
-
+    tree_end(0)
+
+    def sent(own, every, others, sem):
         @pl.when(jnp.logical_not(own))
         def _():
-            wait_bytes(um, uq_send.at[qq])
-
+            wait_bytes(every, sem)
+
+        @pl.when(own)
+        def _():
+            wait_bytes(others, sem)
+
+    home = q == p // 2
+    sent(home, us, us.at[1:NP], u_send.at[0])
+    sent(q % 2 == y // 2, us, us.at[1:NP], ur_send.at[0])
+    sent(q // 2 == x, uq, uq.at[1:4], uq_send.at[0])
+    sent(home, rgp, rgp.at[1:NP], g_send.at[0])
     wait_bytes(vr.at[z, x], vx_send.at[0])
     wait_bytes(vq.at[z, 1:4], vy_send.at[0])
     wait_bytes(vr.at[1:NZ], vr_send.at[0])
     wait_bytes(vq.at[1:NZ], vq_send.at[0])
-    for zz in range(NZ):
-        wait_bytes(xsr.at[zz, 1:4], xr_send.at[zz])
-        wait_bytes(xsq.at[zz], xq_send.at[zz])
-    for u in range(8):
-        wait_bytes(zs.at[u, 1:NP], z_send.at[u])
-    for k in range(NP):
-        own = jnp.logical_and(k == 0, p // 2 == q)
-
-        @pl.when(jnp.logical_not(own))
-        def _():
-            wait_bytes(rgp.at[k], g_send.at[k])
-
+    wait_bytes(xsr.at[:, 1:4], xr_send.at[0])
+    wait_bytes(xsq, xq_send.at[0])
     for h in range(2):
-        for n in range(NS):
-            rows = slice(n * (128 // NS), (n + 1) * (128 // NS))
-            for s in range(4):
-                wait_bytes(rbuf.at[h, s, rows], r_send.at[h, s, n])
-            for s in range(3):
-                wait_bytes(lbuf.at[h, s, rows], l_send.at[h, s, n])
+        wait_bytes(zs.at[4 * h : 4 * h + 4, 1:NP], z_send.at[h])
+    for h in range(2):
+        wait_bytes(tbuf.at[h], t_send.at[h])
 
 
 def shards(receiver_spectra, reference_spectra, receiver_counts, reference_counts, column_station, lag_window, observed):
@@ -564,7 +539,7 @@
             pltpu.VMEM((2, NI, 1152), BF),
             pltpu.VMEM((NP, NI, 1152), BF),
             pltpu.VMEM((4, 2, NI, 1152), BF),
-            pltpu.VMEM((2, 2, 2, NI, 1152), BF),
+            pltpu.VMEM((4, 2, NI, 1152), BF),
             pltpu.VMEM((NZ, 2, 128, 128), BF),
             pltpu.VMEM((NZ, 4, 128, 128), BF),
             pltpu.VMEM((NZ, 4, 2, NI, 256), F32),
@@ -591,14 +566,13 @@
             pltpu.VMEM((8, NP, NG, 16, NJ), BF),
             pltpu.VMEM((NG, 8, NP, 16, NJ), BF),
             pltpu.VMEM((2, NZ, 128, 128), F32),
-            pltpu.VMEM((2, 4, 128, 128), F32),
-            pltpu.VMEM((2, 3, 128, 128), F32),
+            pltpu.VMEM((2, 7, 128, 128), F32),
             pltpu.VMEM((NP, NI, 1024), F32),
             pltpu.VMEM((4, 2, NI, 1024), F32),
-            dma((NI + 2,)), dma((2, 4)), dma((NP,)), dma((2, 4)), dma((4, 2)), dma((4,)), dma((2, 2)),
+            dma((3,)), dma((1,)), dma((1,)), dma((1,)), dma((1,)), dma((1,)), dma((1,)),
             dma((1,)), dma((1,)), dma((1,)), dma((4,)), dma((1,)), dma((NZ, 2)), dma((1,)), dma((NZ, 4)),
-            dma((NZ,)), dma((NZ,)), dma((NZ,)), dma((NZ,)), dma((8,)), dma((8,)),
-            dma((NP,)), dma((4, 2)), dma((2, 4, NS)), dma((2, 4, NS)), dma((2, 3, NS)), dma((2, 3, NS)),
+            dma((1,)), dma((1,)), dma((1,)), dma((1,)), dma((2,)), dma((8,)),
+            dma((1,)), dma((1,)), dma((2,)), dma((2, 7)),
         ],
         compiler_params=pltpu.CompilerParams(
             collective_id=0, has_side_effects=True, vmem_limit_bytes=60 * 1024 * 1024

time: 79.2 us -> 78.8 us (level)
  no operation moved by 1% of the time
where the time goes in v6:
time: 78.8 us; the launch traced here: 78.7 us
  Pallas kernels  76.8 us (97%)
  local copies, waits for them, and re-layouts  1.29 us (2%)
    pallas_call x1, Pallas kernels, shards(): pl.pallas_call(kernel, out_shape=(pltpu.VMEM((NI, 2048), F32), pltpu.VMEM...  76.8 us

profile of v6, /device:TPU:2, one launch (start us, length us, event | category | flops | bytes accessed | tf_op | source)
XLA Modules:
  0.0 78.7 jit_solution(15005215729122955715)
XLA Ops:
  0.6 76.8 %shard_map.104 = (f32[8,2048]{1,0:T(8,128)S(1)}, f32[128,256]{1,0:T(8,128)S(1)}) custom-call(bf16[8,2048]{1,0:T(8,128)(2,1)} %u_ref.1, bf16[128,256]{1,0:T(8,128)(2,1)} %v_ref.1, s32[1,8]{1,0:T(1,128)} %bitcast.5, s32[1,256]{1,0:T(1,128)} %bitcast.3, s32[1,256]{1,0:T(1,128)} %bitcast.4, s32[2,8,256]{2,1,0:T(8,128)} %win_ref.1, bf16[8,256,512]{2,1,0:T(8,128)(2,1)} %obs_hbm.1, ...), custom_call_target="tpu_custom_call" | custom-call | tf_op jit(solution)/shard_map/pallas_call | solution.py:530
  77.4 0.6 copy.13
  78.0 0.7 copy.14

commit v7 on v6

--- a/solution.py
+++ b/solution.py
@@ -190,26 +190,23 @@
     def ahead(s):
         return (z + s) % NZ
 
+    def step(s, buf, recv, pass_to, sub, up):
+        if s <= up:
+            wait_bytes(buf.at[back(s), sub], recv.at[back(s), sub])
+            if s < up:
+                pass_to(back(s), sub, right)
+        if s <= 7 - up:
+            wait_bytes(buf.at[ahead(s), sub], recv.at[ahead(s), sub])
+            if s < 7 - up:
+                pass_to(ahead(s), sub, left)
+
     def step_r(s):
         for k in range(2):
-            sub = (x + k) % 2
-            if s < 4:
-                wait_bytes(vr.at[back(s), sub], vr_recv.at[back(s), sub])
-                if s < 3:
-                    pass_r(back(s), sub, right)
-            wait_bytes(vr.at[ahead(s), sub], vr_recv.at[ahead(s), sub])
-            if s < 4:
-                pass_r(ahead(s), sub, left)
+            step(s, vr, vr_recv, pass_r, (x + k) % 2, 4 - k)
 
     def step_q(s):
         for k in (0, 1, 3, 2):
-            sub = (y + k) % 4
-            wait_bytes(vq.at[back(s), sub], vq_recv.at[back(s), sub])
-            if s < 4:
-                pass_q(back(s), sub, right)
-                wait_bytes(vq.at[ahead(s), sub], vq_recv.at[ahead(s), sub])
-                if s < 3:
-                    pass_q(ahead(s), sub, left)
+            step(s, vq, vq_recv, pass_q, (y + k) % 4, 4 if k < 2 else 3)
 
     row16 = lax.broadcasted_iota(jnp.int32, (16, 256), 0)
     lane256 = lax.broadcasted_iota(jnp.int32, (16, 256), 1)
@@ -337,6 +334,8 @@
     step_q(3)
     crossings(cross_q, 5, 7)
     reorder(from_q, mq_ref)
+    step_q(4)
+    crossings(cross_q, 7, 8)
 
     TB = 128
     def pairs(u, got, table):
@@ -372,8 +371,6 @@
 
     wait_bytes(xsr.at[:, 1:4], xr_recv.at[0])
     lax.fori_loop(0, 4, pairs_r, 0)
-    step_q(4)
-    crossings(cross_q, 7, 8)
     wait_bytes(xsq, xq_recv.at[0])
     lax.fori_loop(0, 4, pairs_q, 0)
 
@@ -416,25 +413,39 @@
                 part = part + w[h, 2 * g : 2 * g + 2]
             w[h, 2 * g : 2 * g + 2] = part
 
-    def toward(n, src, dst, h, to):
-        remote(src, dst, t_send.at[h], t_recv.at[h, n], p * NZ + (z + NZ + to) % NZ, q).start()
+    def toward(n, src, h, part, to):
+        rows = slice(part * 64, (part + 1) * 64)
+        remote(
+            src.at[rows], tbuf.at[h, n, rows], t_send.at[h], t_recv.at[h, n, part],
+            p * NZ + (z + NZ + to) % NZ, q,
+        ).start()
+
+    def landed(n, h, part):
+        wait_bytes(tbuf.at[h, n, part * 64 : (part + 1) * 64], t_recv.at[h, n, part])
 
     def tree_start(h):
-        for n, m, to in ((0, 4, 2), (1, 3, 1), (2, 5, -1), (3, 1, 1), (4, 7, -1)):
-            toward(n, w.at[h, (z + m) % NZ], tbuf.at[h, n], h, to)
+        for part in range(2):
+            for n, m, to in ((0, 4, 2), (2, 5, -1), (1, 3, 1)):
+                toward(n, w.at[h, (z + m) % NZ], h, part, to)
+        for part in range(2):
+            for n, m, to in ((3, 1, 1), (4, 7, -1)):
+                toward(n, w.at[h, (z + m) % NZ], h, part, to)
 
     def tree_middle(h):
-        wait_bytes(tbuf.at[h, 2], t_recv.at[h, 2])
-        tbuf[h, 2] = tbuf[h, 2] + w[h, (z + 6) % NZ]
-        toward(6, tbuf.at[h, 2], tbuf.at[h, 6], h, -2)
-        wait_bytes(tbuf.at[h, 1], t_recv.at[h, 1])
-        wait_bytes(tbuf.at[h, 0], t_recv.at[h, 0])
-        tbuf[h, 0] = tbuf[h, 0] + (tbuf[h, 1] + w[h, (z + 2) % NZ])
-        toward(5, tbuf.at[h, 0], tbuf.at[h, 5], h, 2)
+        for part in range(2):
+            rows = slice(part * 64, (part + 1) * 64)
+            landed(2, h, part)
+            tbuf[h, 2, rows] = tbuf[h, 2, rows] + w[h, (z + 6) % NZ, rows]
+            toward(6, tbuf.at[h, 2], h, part, -2)
+            landed(1, h, part)
+            landed(0, h, part)
+            tbuf[h, 0, rows] = tbuf[h, 0, rows] + (tbuf[h, 1, rows] + w[h, (z + 2) % NZ, rows])
+            toward(5, tbuf.at[h, 0], h, part, 2)
 
     def tree_end(h):
         for n in (3, 4, 6, 5):
-            wait_bytes(tbuf.at[h, n], t_recv.at[h, n])
+            for part in range(2):
+                landed(n, h, part)
         done = (w[h, z] + tbuf[h, 3]) + (tbuf[h, 4] + tbuf[h, 6]) + tbuf[h, 5]
         cols = slice(h * 128, (h + 1) * 128)
         wg_out[:, cols] = jnp.where(row_mask[:, cols], done, 0.0)
@@ -572,7 +583,7 @@
             dma((3,)), dma((1,)), dma((1,)), dma((1,)), dma((1,)), dma((1,)), dma((1,)),
             dma((1,)), dma((1,)), dma((1,)), dma((4,)), dma((1,)), dma((NZ, 2)), dma((1,)), dma((NZ, 4)),
             dma((1,)), dma((1,)), dma((1,)), dma((1,)), dma((2,)), dma((8,)),
-            dma((1,)), dma((1,)), dma((2,)), dma((2, 7)),
+            dma((1,)), dma((1,)), dma((2,)), dma((2, 7, 2)),
         ],
         compiler_params=pltpu.CompilerParams(
             collective_id=0, has_side_effects=True, vmem_limit_bytes=60 * 1024 * 1024

time: 78.8 us -> 73 us (0.926)
  Pallas kernels: 76.8 us -> 70.9 us
    pallas_call x1, Pallas kernels: 76.8 us -> 70.9 us  [shards(): pl.pallas_call(kernel, out_shape=(pltpu.VMEM((NI, 2048), F32), pltpu.VMEM...]
where the time goes in v7:
time: 73 us; the launch traced here: 72.9 us
  Pallas kernels  70.9 us (97%)
  local copies, waits for them, and re-layouts  1.29 us (2%)
    pallas_call x1, Pallas kernels, shards(): pl.pallas_call(kernel, out_shape=(pltpu.VMEM((NI, 2048), F32), pltpu.VMEM...  70.9 us

profile of v7, /device:TPU:2, one launch (start us, length us, event | category | flops | bytes accessed | tf_op | source)
XLA Modules:
  0.0 72.9 jit_solution(14033977948174212056)
XLA Ops:
  0.6 70.9 %shard_map.104 = (f32[8,2048]{1,0:T(8,128)S(1)}, f32[128,256]{1,0:T(8,128)S(1)}) custom-call(bf16[8,2048]{1,0:T(8,128)(2,1)} %u_ref.1, bf16[128,256]{1,0:T(8,128)(2,1)} %v_ref.1, s32[1,8]{1,0:T(1,128)} %bitcast.5, s32[1,256]{1,0:T(1,128)} %bitcast.3, s32[1,256]{1,0:T(1,128)} %bitcast.4, s32[2,8,256]{2,1,0:T(8,128)} %win_ref.1, bf16[8,256,512]{2,1,0:T(8,128)(2,1)} %obs_hbm.1, ...), custom_call_target="tpu_custom_call" | custom-call | tf_op jit(solution)/shard_map/pallas_call | solution.py:541
  71.6 0.6 copy.13
  72.2 0.7 copy.14

commit v8 on v7

--- a/solution.py
+++ b/solution.py
@@ -37,8 +37,9 @@
 
 
 def kernel(
-    u_ref, v_ref, rc_ref, fc_ref, cs_ref, win_ref, obs_hbm, m_hbm, mt_hbm,
+    u_hbm, v_hbm, rc_hbm, fc_hbm, cs_hbm, win_hbm, obs_hbm, m_hbm, mt_hbm,
     rg_out, wg_out,
+    u_ref, v_ref, rc_ref, fc_ref, cs_ref, win_ref,
     um, us, ur, uq, vr, vq, ucr, ucq, bw, scr, scq, bt, bb, ninv, first, last,
     obs, m_ref, mt_ref, mq_ref, mr_ref, obst, xsr, xrr, xsq, xrq, gs, zs, zr,
     w, tbuf, rgp, rgr,
@@ -72,6 +73,11 @@
     def wait_bytes(ref, sem):
         pltpu.make_async_copy(ref, ref, sem).wait()
 
+    small = ((u_hbm, u_ref), (v_hbm, v_ref), (rc_hbm, rc_ref), (fc_hbm, fc_ref), (cs_hbm, cs_ref), (win_hbm, win_ref))
+    firsts = [pltpu.make_async_copy(src, dst, in_sem.at[3 + n]) for n, (src, dst) in enumerate(small)]
+    for load in firsts:
+        load.start()
+
     barrier = pltpu.get_barrier_semaphore()
     for k in range(NP):
         for dq in range(4):
@@ -85,6 +91,9 @@
     loads.append(pltpu.make_async_copy(m_hbm, m_ref, in_sem.at[2]))
     for load in loads:
         load.start()
+
+    for load in firsts:
+        load.wait()
 
     eye = lax.broadcasted_iota(jnp.int32, (NI, NI), 0) == lax.broadcasted_iota(jnp.int32, (NI, NI), 1)
     rcounts = jnp.sum(jnp.where(eye, rc_ref[...].astype(F32), 0.0), axis=1, keepdims=True)
@@ -190,23 +199,24 @@
     def ahead(s):
         return (z + s) % NZ
 
-    def step(s, buf, recv, pass_to, sub, up):
-        if s <= up:
-            wait_bytes(buf.at[back(s), sub], recv.at[back(s), sub])
-            if s < up:
-                pass_to(back(s), sub, right)
-        if s <= 7 - up:
-            wait_bytes(buf.at[ahead(s), sub], recv.at[ahead(s), sub])
-            if s < 7 - up:
-                pass_to(ahead(s), sub, left)
+    def step(s, buf, recv, pass_to, sub, up, down, beside=False):
+        for zz, most, to in ((back(s), up, right), (ahead(s), down, left)):
+            if s == 4 and most < 4 and (to is left or down == 4):
+                continue
+            wait_bytes(buf.at[zz, sub], recv.at[zz, sub])
+            if s < most:
+                pass_to(zz, sub, to)
+            if beside and s > 2:
+                for k in (1, 3):
+                    pass_to(zz, sub, (x * 4 + (y + k) % 4) * NZ + z)
 
     def step_r(s):
         for k in range(2):
-            step(s, vr, vr_recv, pass_r, (x + k) % 2, 4 - k)
+            step(s, vr, vr_recv, pass_r, (x + k) % 2, 4 - k, 3 + k)
 
     def step_q(s):
-        for k in (0, 1, 3, 2):
-            step(s, vq, vq_recv, pass_q, (y + k) % 4, 4 if k < 2 else 3)
+        for k, up, down in ((0, 4, 3), (2, 3, 4), (1, 2, 2), (3, 2, 2)):
+            step(s, vq, vq_recv, pass_q, (y + k) % 4, up, down, k == 0)
 
     row16 = lax.broadcasted_iota(jnp.int32, (16, 256), 0)
     lane256 = lax.broadcasted_iota(jnp.int32, (16, 256), 1)
@@ -544,9 +554,15 @@
             pltpu.VMEM((NI, 2048), F32),
             pltpu.VMEM((128, NJ), F32),
         ),
-        in_specs=[vmem] * 6 + [hbm] * 3,
+        in_specs=[hbm] * 9,
         out_specs=(pl.BlockSpec(memory_space=pltpu.MemorySpace.VMEM), pl.BlockSpec(memory_space=pltpu.MemorySpace.VMEM)),
         scratch_shapes=[
+            pltpu.VMEM((NI, 2048), BF),
+            pltpu.VMEM((128, NJ), BF),
+            pltpu.VMEM((1, NI), jnp.int32),
+            pltpu.VMEM((1, NJ), jnp.int32),
+            pltpu.VMEM((1, NJ), jnp.int32),
+            pltpu.VMEM((2, NI, NJ), jnp.int32),
             pltpu.VMEM((2, NI, 1152), BF),
             pltpu.VMEM((NP, NI, 1152), BF),
             pltpu.VMEM((4, 2, NI, 1152), BF),
@@ -580,7 +596,7 @@
             pltpu.VMEM((2, 7, 128, 128), F32),
             pltpu.VMEM((NP, NI, 1024), F32),
             pltpu.VMEM((4, 2, NI, 1024), F32),
-            dma((3,)), dma((1,)), dma((1,)), dma((1,)), dma((1,)), dma((1,)), dma((1,)),
+            dma((9,)), dma((1,)), dma((1,)), dma((1,)), dma((1,)), dma((1,)), dma((1,)),
             dma((1,)), dma((1,)), dma((1,)), dma((4,)), dma((1,)), dma((NZ, 2)), dma((1,)), dma((NZ, 4)),
             dma((1,)), dma((1,)), dma((1,)), dma((1,)), dma((2,)), dma((8,)),
             dma((1,)), dma((1,)), dma((2,)), dma((2, 7, 2)),

time: 73 us -> 76.8 us (1.052)
  Pallas kernels: 70.9 us -> 74.3 us
    pallas_call x1, Pallas kernels: 70.9 us -> 74.3 us  [shards(): pl.pallas_call(kernel, out_shape=(pltpu.VMEM((NI, 2048), F32), pltpu.VMEM...]
where the time goes in v8:
time: 76.8 us; the launch traced here: 76.2 us
  Pallas kernels  74.3 us (97%)
  local copies, waits for them, and re-layouts  1.29 us (2%)
    pallas_call x1, Pallas kernels, shards(): pl.pallas_call(kernel, out_shape=(pltpu.VMEM((NI, 2048), F32), pltpu.VMEM...  74.3 us

profile of v8, /device:TPU:2, one launch (start us, length us, event | category | flops | bytes accessed | tf_op | source)
XLA Modules:
  0.0 76.2 jit_solution(14338018012077050954)
XLA Ops:
  0.6 74.3 %shard_map.104 = (f32[8,2048]{1,0:T(8,128)S(1)}, f32[128,256]{1,0:T(8,128)S(1)}) custom-call(bf16[8,2048]{1,0:T(8,128)(2,1)} %u_hbm.1, bf16[128,256]{1,0:T(8,128)(2,1)} %v_hbm.1, s32[1,8]{1,0:T(1,128)} %bitcast.5, s32[1,256]{1,0:T(1,128)} %bitcast.3, s32[1,256]{1,0:T(1,128)} %bitcast.4, s32[2,8,256]{2,1,0:T(8,128)} %win_hbm.1, bf16[8,256,512]{2,1,0:T(8,128)(2,1)} %obs_hbm.1, ...), custom_call_target="tpu_custom_call" | custom-call | tf_op jit(solution)/shard_map/pallas_call | solution.py:551
  74.9 0.6 copy.13
  75.6 0.7 copy.14

commit v9 on v7

--- a/solution.py
+++ b/solution.py
@@ -37,8 +37,9 @@
 
 
 def kernel(
-    u_ref, v_ref, rc_ref, fc_ref, cs_ref, win_ref, obs_hbm, m_hbm, mt_hbm,
+    u_hbm, v_hbm, rc_hbm, fc_hbm, cs_hbm, win_hbm, obs_hbm, m_hbm, mt_hbm,
     rg_out, wg_out,
+    u_ref, v_ref, rc_ref, fc_ref, cs_ref, win_ref,
     um, us, ur, uq, vr, vq, ucr, ucq, bw, scr, scq, bt, bb, ninv, first, last,
     obs, m_ref, mt_ref, mq_ref, mr_ref, obst, xsr, xrr, xsq, xrq, gs, zs, zr,
     w, tbuf, rgp, rgr,
@@ -72,6 +73,11 @@
     def wait_bytes(ref, sem):
         pltpu.make_async_copy(ref, ref, sem).wait()
 
+    small = ((u_hbm, u_ref), (v_hbm, v_ref), (rc_hbm, rc_ref), (fc_hbm, fc_ref), (cs_hbm, cs_ref), (win_hbm, win_ref))
+    firsts = [pltpu.make_async_copy(src, dst, in_sem.at[3 + n]) for n, (src, dst) in enumerate(small)]
+    for load in firsts:
+        load.start()
+
     barrier = pltpu.get_barrier_semaphore()
     for k in range(NP):
         for dq in range(4):
@@ -85,6 +91,9 @@
     loads.append(pltpu.make_async_copy(m_hbm, m_ref, in_sem.at[2]))
     for load in loads:
         load.start()
+
+    for load in firsts:
+        load.wait()
 
     eye = lax.broadcasted_iota(jnp.int32, (NI, NI), 0) == lax.broadcasted_iota(jnp.int32, (NI, NI), 1)
     rcounts = jnp.sum(jnp.where(eye, rc_ref[...].astype(F32), 0.0), axis=1, keepdims=True)
@@ -334,8 +343,6 @@
     step_q(3)
     crossings(cross_q, 5, 7)
     reorder(from_q, mq_ref)
-    step_q(4)
-    crossings(cross_q, 7, 8)
 
     TB = 128
     def pairs(u, got, table):
@@ -355,22 +362,42 @@
         for b in range(4):
             back = jnp.dot(m_ref[b * 128 : (b + 1) * 128, :], gs[...], preferred_element_type=F32)
             zs[u, 2 * b : 2 * b + 2] = (back * scale).astype(BF).reshape(2, NG, 16, NJ)
-        for k in (4, 5, 7, 6, 1, 3, 2):
+        zr[:, u, 0] = zs[u, p]
+
+    def hand_out(u, across, beside):
+        todo = [(1, k) for k in (0, 1, 3, 2) if across] + [(0, k) for k in (1, 3, 2) if beside]
+        for xx, k in todo:
+            peer = ((x + xx) % 2) * 4 + (y + k) % 4
             remote(
-                zs.at[u, (p + k) % NP], zr.at[:, u, NP - k], z_send.at[u // 4], z_recv.at[u], plane(k), q
+                zs.at[u, peer], zr.at[:, u, (p - peer + NP) % NP], z_send.at[u // 4], z_recv.at[u],
+                peer * NZ + z, q,
             ).start()
-        zr[:, u, 0] = zs[u, p]
 
     def pairs_r(ii, c):
         pairs(4 + ii, xrr[ii].reshape(2 * F, NJ), mr_ref)
+        hand_out(4 + ii, True, True)
+        return c
+
+    def pairs_y(ii, c):
+        pairs(4 + ii, xrr[ii].reshape(2 * F, NJ), mr_ref)
+        hand_out(4 + ii, False, True)
+        return c
+
+    def hand_x(ii, c):
+        hand_out(4 + ii, True, False)
         return c
 
     def pairs_q(ii, c):
         pairs(ii, xrq[ii].reshape(2 * F, NJ), mq_ref)
+        hand_out(ii, True, True)
         return c
 
     wait_bytes(xsr.at[:, 1:4], xr_recv.at[0])
-    lax.fori_loop(0, 4, pairs_r, 0)
+    lax.fori_loop(0, 2, pairs_y, 0)
+    step_q(4)
+    crossings(cross_q, 7, 8)
+    lax.fori_loop(0, 2, hand_x, 0)
+    lax.fori_loop(2, 4, pairs_r, 0)
     wait_bytes(xsq, xq_recv.at[0])
     lax.fori_loop(0, 4, pairs_q, 0)
 
@@ -544,9 +571,15 @@
             pltpu.VMEM((NI, 2048), F32),
             pltpu.VMEM((128, NJ), F32),
         ),
-        in_specs=[vmem] * 6 + [hbm] * 3,
+        in_specs=[hbm] * 9,
         out_specs=(pl.BlockSpec(memory_space=pltpu.MemorySpace.VMEM), pl.BlockSpec(memory_space=pltpu.MemorySpace.VMEM)),
         scratch_shapes=[
+            pltpu.VMEM((NI, 2048), BF),
+            pltpu.VMEM((128, NJ), BF),
+            pltpu.VMEM((1, NI), jnp.int32),
+            pltpu.VMEM((1, NJ), jnp.int32),
+            pltpu.VMEM((1, NJ), jnp.int32),
+            pltpu.VMEM((2, NI, NJ), jnp.int32),
             pltpu.VMEM((2, NI, 1152), BF),
             pltpu.VMEM((NP, NI, 1152), BF),
             pltpu.VMEM((4, 2, NI, 1152), BF),
@@ -580,7 +613,7 @@
             pltpu.VMEM((2, 7, 128, 128), F32),
             pltpu.VMEM((NP, NI, 1024), F32),
             pltpu.VMEM((4, 2, NI, 1024), F32),
-            dma((3,)), dma((1,)), dma((1,)), dma((1,)), dma((1,)), dma((1,)), dma((1,)),
+            dma((9,)), dma((1,)), dma((1,)), dma((1,)), dma((1,)), dma((1,)), dma((1,)),
             dma((1,)), dma((1,)), dma((1,)), dma((4,)), dma((1,)), dma((NZ, 2)), dma((1,)), dma((NZ, 4)),
             dma((1,)), dma((1,)), dma((1,)), dma((1,)), dma((2,)), dma((8,)),
             dma((1,)), dma((1,)), dma((2,)), dma((2, 7, 2)),

time: 73 us -> 73.7 us (level)
  Pallas kernels: 70.9 us -> 71.7 us
    pallas_call x1, Pallas kernels: 70.9 us -> 71.7 us  [shards(): pl.pallas_call(kernel, out_shape=(pltpu.VMEM((NI, 2048), F32), pltpu.VMEM...]
where the time goes in v9:
time: 73.7 us; the launch traced here: 73.6 us
  Pallas kernels  71.7 us (97%)
  local copies, waits for them, and re-layouts  1.29 us (2%)
    pallas_call x1, Pallas kernels, shards(): pl.pallas_call(kernel, out_shape=(pltpu.VMEM((NI, 2048), F32), pltpu.VMEM...  71.7 us

profile of v9, /device:TPU:2, one launch (start us, length us, event | category | flops | bytes accessed | tf_op | source)
XLA Modules:
  0.0 73.6 jit_solution(3675129209922520074)
XLA Ops:
  0.6 71.7 %shard_map.104 = (f32[8,2048]{1,0:T(8,128)S(1)}, f32[128,256]{1,0:T(8,128)S(1)}) custom-call(bf16[8,2048]{1,0:T(8,128)(2,1)} %u_hbm.1, bf16[128,256]{1,0:T(8,128)(2,1)} %v_hbm.1, s32[1,8]{1,0:T(1,128)} %bitcast.5, s32[1,256]{1,0:T(1,128)} %bitcast.3, s32[1,256]{1,0:T(1,128)} %bitcast.4, s32[2,8,256]{2,1,0:T(8,128)} %win_hbm.1, bf16[8,256,512]{2,1,0:T(8,128)(2,1)} %obs_hbm.1, ...), custom_call_target="tpu_custom_call" | custom-call | tf_op jit(solution)/shard_map/pallas_call | solution.py:568
  72.3 0.6 copy.13
  72.9 0.7 copy.14

commit v10 on v7

--- a/solution.py
+++ b/solution.py
@@ -37,8 +37,9 @@
 
 
 def kernel(
-    u_ref, v_ref, rc_ref, fc_ref, cs_ref, win_ref, obs_hbm, m_hbm, mt_hbm,
+    u_hbm, v_hbm, rc_hbm, fc_hbm, cs_hbm, win_hbm, obs_hbm, m_hbm, mt_hbm,
     rg_out, wg_out,
+    u_ref, v_ref, rc_ref, fc_ref, cs_ref, win_ref,
     um, us, ur, uq, vr, vq, ucr, ucq, bw, scr, scq, bt, bb, ninv, first, last,
     obs, m_ref, mt_ref, mq_ref, mr_ref, obst, xsr, xrr, xsq, xrq, gs, zs, zr,
     w, tbuf, rgp, rgr,
@@ -72,6 +73,11 @@
     def wait_bytes(ref, sem):
         pltpu.make_async_copy(ref, ref, sem).wait()
 
+    small = ((u_hbm, u_ref), (v_hbm, v_ref), (rc_hbm, rc_ref), (fc_hbm, fc_ref), (cs_hbm, cs_ref), (win_hbm, win_ref))
+    firsts = [pltpu.make_async_copy(src, dst, in_sem.at[3 + n]) for n, (src, dst) in enumerate(small)]
+    for load in firsts:
+        load.start()
+
     barrier = pltpu.get_barrier_semaphore()
     for k in range(NP):
         for dq in range(4):
@@ -85,6 +91,9 @@
     loads.append(pltpu.make_async_copy(m_hbm, m_ref, in_sem.at[2]))
     for load in loads:
         load.start()
+
+    for load in firsts:
+        load.wait()
 
     eye = lax.broadcasted_iota(jnp.int32, (NI, NI), 0) == lax.broadcasted_iota(jnp.int32, (NI, NI), 1)
     rcounts = jnp.sum(jnp.where(eye, rc_ref[...].astype(F32), 0.0), axis=1, keepdims=True)
@@ -355,7 +364,7 @@
         for b in range(4):
             back = jnp.dot(m_ref[b * 128 : (b + 1) * 128, :], gs[...], preferred_element_type=F32)
             zs[u, 2 * b : 2 * b + 2] = (back * scale).astype(BF).reshape(2, NG, 16, NJ)
-        for k in (4, 5, 7, 6, 1, 3, 2):
+        for k in range(1, NP):
             remote(
                 zs.at[u, (p + k) % NP], zr.at[:, u, NP - k], z_send.at[u // 4], z_recv.at[u], plane(k), q
             ).start()
@@ -544,9 +553,15 @@
             pltpu.VMEM((NI, 2048), F32),
             pltpu.VMEM((128, NJ), F32),
         ),
-        in_specs=[vmem] * 6 + [hbm] * 3,
+        in_specs=[hbm] * 9,
         out_specs=(pl.BlockSpec(memory_space=pltpu.MemorySpace.VMEM), pl.BlockSpec(memory_space=pltpu.MemorySpace.VMEM)),
         scratch_shapes=[
+            pltpu.VMEM((NI, 2048), BF),
+            pltpu.VMEM((128, NJ), BF),
+            pltpu.VMEM((1, NI), jnp.int32),
+            pltpu.VMEM((1, NJ), jnp.int32),
+            pltpu.VMEM((1, NJ), jnp.int32),
+            pltpu.VMEM((2, NI, NJ), jnp.int32),
             pltpu.VMEM((2, NI, 1152), BF),
             pltpu.VMEM((NP, NI, 1152), BF),
             pltpu.VMEM((4, 2, NI, 1152), BF),
@@ -580,7 +595,7 @@
             pltpu.VMEM((2, 7, 128, 128), F32),
             pltpu.VMEM((NP, NI, 1024), F32),
             pltpu.VMEM((4, 2, NI, 1024), F32),
-            dma((3,)), dma((1,)), dma((1,)), dma((1,)), dma((1,)), dma((1,)), dma((1,)),
+            dma((9,)), dma((1,)), dma((1,)), dma((1,)), dma((1,)), dma((1,)), dma((1,)),
             dma((1,)), dma((1,)), dma((1,)), dma((4,)), dma((1,)), dma((NZ, 2)), dma((1,)), dma((NZ, 4)),
             dma((1,)), dma((1,)), dma((1,)), dma((1,)), dma((2,)), dma((8,)),
             dma((1,)), dma((1,)), dma((2,)), dma((2, 7, 2)),

time: 73 us -> 71.6 us (0.981)
  Pallas kernels: 70.9 us -> 69.1 us
    pallas_call x1, Pallas kernels: 70.9 us -> 69.1 us  [shards(): pl.pallas_call(kernel, out_shape=(pltpu.VMEM((NI, 2048), F32), pltpu.VMEM...]
where the time goes in v10:
time: 71.6 us; the launch traced here: 71 us
  Pallas kernels  69.1 us (97%)
  local copies, waits for them, and re-layouts  1.29 us (2%)
    pallas_call x1, Pallas kernels, shards(): pl.pallas_call(kernel, out_shape=(pltpu.VMEM((NI, 2048), F32), pltpu.VMEM...  69.1 us

profile of v10, /device:TPU:2, one launch (start us, length us, event | category | flops | bytes accessed | tf_op | source)
XLA Modules:
  0.0 71.0 jit_solution(11282133446492333865)
XLA Ops:
  0.6 69.1 %shard_map.104 = (f32[8,2048]{1,0:T(8,128)S(1)}, f32[128,256]{1,0:T(8,128)S(1)}) custom-call(bf16[8,2048]{1,0:T(8,128)(2,1)} %u_hbm.1, bf16[128,256]{1,0:T(8,128)(2,1)} %v_hbm.1, s32[1,8]{1,0:T(1,128)} %bitcast.5, s32[1,256]{1,0:T(1,128)} %bitcast.3, s32[1,256]{1,0:T(1,128)} %bitcast.4, s32[2,8,256]{2,1,0:T(8,128)} %win_hbm.1, bf16[8,256,512]{2,1,0:T(8,128)(2,1)} %obs_hbm.1, ...), custom_call_target="tpu_custom_call" | custom-call | tf_op jit(solution)/shard_map/pallas_call | solution.py:550
  69.8 0.6 copy.13
  70.4 0.7 copy.14

commit v11 on v10

--- a/solution.py
+++ b/solution.py
@@ -491,7 +491,6 @@
     arrived(2)
     receivers(2)
     sums(0, 0, 3)
-    tree_end(1)
     arrived(3)
     sums(0, 3, 4)
     tree_start(0)
@@ -507,6 +506,7 @@
         def _():
             pltpu.make_async_copy(rgp.at[k], rgr.at[q, p % 2], g_recv.at[0]).start()
 
+    tree_end(1)
     tree_middle(0)
     wait_bytes(rgr, g_recv.at[0])
     for half in range(2):

time: 71.6 us -> 70.8 us (0.989)
  no operation moved by 1% of the time
where the time goes in v11:
time: 70.8 us; the launch traced here: 70.7 us
  Pallas kernels  68.8 us (97%)
  local copies, waits for them, and re-layouts  1.29 us (2%)
    pallas_call x1, Pallas kernels, shards(): pl.pallas_call(kernel, out_shape=(pltpu.VMEM((NI, 2048), F32), pltpu.VMEM...  68.8 us

profile of v11, /device:TPU:2, one launch (start us, length us, event | category | flops | bytes accessed | tf_op | source)
XLA Modules:
  0.0 70.7 jit_solution(5291476353805826006)
XLA Ops:
  0.6 68.8 %shard_map.104 = (f32[8,2048]{1,0:T(8,128)S(1)}, f32[128,256]{1,0:T(8,128)S(1)}) custom-call(bf16[8,2048]{1,0:T(8,128)(2,1)} %u_hbm.1, bf16[128,256]{1,0:T(8,128)(2,1)} %v_hbm.1, s32[1,8]{1,0:T(1,128)} %bitcast.5, s32[1,256]{1,0:T(1,128)} %bitcast.3, s32[1,256]{1,0:T(1,128)} %bitcast.4, s32[2,8,256]{2,1,0:T(8,128)} %win_hbm.1, bf16[8,256,512]{2,1,0:T(8,128)(2,1)} %obs_hbm.1, ...), custom_call_target="tpu_custom_call" | custom-call | tf_op jit(solution)/shard_map/pallas_call | solution.py:550
  69.4 0.6 copy.13
  70.1 0.7 copy.14

commit v12 on v11

--- a/solution.py
+++ b/solution.py
@@ -185,14 +185,6 @@
         wait_bytes(vq.at[z, yy], vy_recv.at[yy])
         pass_q(z, yy, right)
         pass_q(z, yy, left)
-    for half in range(2):
-        for qq in range(4):
-            pp = 2 * q + half
-            rr = pp * NZ + z
-            own = jnp.logical_and(rr == r, qq == q)
-            slot = (p - pp + NP) % NP
-            give(own, um.at[half], us.at[slot], u_send.at[0], u_recv.at[0], rr, qq)
-
     def back(s):
         return (z + NZ - s) % NZ
 
@@ -319,6 +311,13 @@
     wait_bytes(uq, uq_recv.at[0])
     lax.fori_loop(0, 2, ready_q, 0)
     crossings(cross_q, 0, 3)
+    for half in range(2):
+        for qq in range(4):
+            pp = 2 * q + half
+            rr = pp * NZ + z
+            own = jnp.logical_and(rr == r, qq == q)
+            slot = (p - pp + NP) % NP
+            give(own, um.at[half], us.at[slot], u_send.at[0], u_recv.at[0], rr, qq)
     step_r(3)
     crossings(cross_r, 5, 7)
     step_q(2)

time: 70.8 us -> 70.6 us (level)
  no operation moved by 1% of the time
where the time goes in v12:
time: 70.6 us; the launch traced here: 70.5 us
  Pallas kernels  68.6 us (97%)
  local copies, waits for them, and re-layouts  1.29 us (2%)
    pallas_call x1, Pallas kernels, shards(): pl.pallas_call(kernel, out_shape=(pltpu.VMEM((NI, 2048), F32), pltpu.VMEM...  68.6 us

profile of v12, /device:TPU:2, one launch (start us, length us, event | category | flops | bytes accessed | tf_op | source)
XLA Modules:
  0.0 70.5 jit_solution(3050265503502899147)
XLA Ops:
  0.6 68.6 %shard_map.104 = (f32[8,2048]{1,0:T(8,128)S(1)}, f32[128,256]{1,0:T(8,128)S(1)}) custom-call(bf16[8,2048]{1,0:T(8,128)(2,1)} %u_hbm.1, bf16[128,256]{1,0:T(8,128)(2,1)} %v_hbm.1, s32[1,8]{1,0:T(1,128)} %bitcast.5, s32[1,256]{1,0:T(1,128)} %bitcast.3, s32[1,256]{1,0:T(1,128)} %bitcast.4, s32[2,8,256]{2,1,0:T(8,128)} %win_hbm.1, bf16[8,256,512]{2,1,0:T(8,128)(2,1)} %obs_hbm.1, ...), custom_call_target="tpu_custom_call" | custom-call | tf_op jit(solution)/shard_map/pallas_call | solution.py:549
  69.2 0.6 copy.13
  69.8 0.7 copy.14
